TPU v7x, 32 devices: a whole 2x2x4 slice. The times are simulated.
32 devices in a mesh: rep: 16 (over z, x, core), shard: 2 (over y).
Axes of the slice: x: 2, y: 2, z: 4, core: 2. Of those that a mesh axis runs over, the one named last changes fastest.
Arguments:
- tokens: bfloat16 [2, 12288, 768], P(None, ('rep', 'shard')), may hold values from -6 to 6
- cotangent: bfloat16 [2, 12288, 768], P(None, ('rep', 'shard')), may hold values from -6 to 6
- seq_lengths: int32 [2, 16, 2], P(None, 'rep'), may hold values from 0 to 768, as said below
- w_query: bfloat16 [768, 768], P('shard'), may hold values from -0.21875 to 0.21875
- b_query: bfloat16 [768], P('shard'), may hold values from -1.5 to 1.5
- w_key: bfloat16 [768, 768], P('shard'), may hold values from -0.21875 to 0.21875
- w_value: bfloat16 [768, 768], P('shard'), may hold values from -0.21875 to 0.21875
- b_value: bfloat16 [768], P('shard'), may hold values from -0.5 to 0.5
- w_attn: bfloat16 [768, 768], P('shard'), may hold values from -3 to 3
- b_attn: bfloat16 [768], P('shard'), may hold values from -1 to 1
- norm_gain: bfloat16 [768], P('shard'), may hold values from 0.5 to 1.5
- norm_bias: bfloat16 [768], P('shard'), may hold values from -1 to 1
- w_up: bfloat16 [768, 3072], P('shard'), may hold values from -0.21875 to 0.21875
- b_up: bfloat16 [3072], P('shard'), may hold values from -1.5 to 1.5
- w_down: bfloat16 [3072, 768], P('shard'), may hold values from -0.109375 to 0.109375
- b_down: bfloat16 [768], P('shard'), may hold values from -1 to 1
- out_gain: bfloat16 [768], P('shard'), may hold values from 0.5 to 1.5
- out_bias: bfloat16 [768], P('shard'), may hold values from -1 to 1
Outputs:
- layer_out: bfloat16 [2, 12288, 768], P(None, ('rep', 'shard'))
- tokens_grad: bfloat16 [2, 12288, 768], P(None, ('rep', 'shard'))
- grad_w_query: float32 [768, 768], P('shard')
- grad_b_query: float32 [768], P('shard')
- grad_w_key: float32 [768, 768], P('shard')
- grad_w_value: float32 [768, 768], P('shard')
- grad_b_value: float32 [768], P('shard')
- grad_w_attn: float32 [768, 768], P('shard')
- grad_b_attn: float32 [768], P('shard')
- grad_norm_gain: float32 [768], P('shard')
- grad_norm_bias: float32 [768], P('shard')
- grad_w_up: float32 [768, 3072], P('shard')
- grad_b_up: float32 [3072], P('shard')
- grad_w_down: float32 [3072, 768], P('shard')
- grad_b_down: float32 [768], P('shard')
- grad_out_gain: float32 [768], P('shard')
- grad_out_bias: float32 [768], P('shard')
Inputs may be any that keep to these rules, and one draw needn't show every extreme that they name: `seq_lengths`: each row gives the lengths of 1 sequence in their order in the group, exactly one sequence of 768 tokens filling the group with a padding length of 0 (1024 exceeds the group); each row sums to 768.
All inputs are finite; a program needn't handle non-finite values.
Results may differ from a plain program's by a relative error of at most 0.02.
Values may be sent and summed in bfloat16 or wider, within the bound.
A program may use at most 192 MiB of HBM per device.

v0:
```python
import functools

import jax
import jax.numpy as jnp
from jax import lax
from jax.experimental import pallas as pl
from jax.experimental.pallas import tpu as pltpu
from jax.sharding import PartitionSpec as P

D = 768
H = 12
DH = 64
PAIR = 2 * DH
EPS = 1e-12
BIG = 1e30
SCALE = DH ** (-0.5)
ROWS = 256
f32 = jnp.float32
bf16 = jnp.bfloat16


def mm(left, right):
    return jnp.dot(left, right, preferred_element_type=f32)


def mm_nt(left, right):
    return lax.dot_general(left, right, (((1,), (1,)), ((), ())), preferred_element_type=f32)


def mm_tn(left, right):
    return lax.dot_general(left, right, (((0,), (0,)), ((), ())), preferred_element_type=f32)


def segment_ids(row, count):
    bounds = jnp.cumsum(row[:-1])
    places = jnp.arange(count, dtype=jnp.int32)
    return jnp.sum((places[:, None] >= bounds[None, :]).astype(jnp.int32), axis=1)


def mask_columns(ids):
    first = (ids == 0).astype(f32)[:, None]
    other = 1.0 - first
    lane = lax.broadcasted_iota(jnp.int32, (1, PAIR), 1) % DH
    on_query = jnp.where(lane == 0, -BIG * first, jnp.where(lane == 1, -BIG * other, 0.0))
    on_key = jnp.where(lane == 0, other, jnp.where(lane == 1, first, 0.0))
    return on_query.astype(bf16), on_key.astype(bf16)


def forward_heads(q_ref, k_ref, v_ref, mq_ref, mk_ref, attn_ref, lse_ref):
    lane = lax.broadcasted_iota(jnp.int32, (1, PAIR), 1)
    low = lane < DH
    keys, values, mk = k_ref[...], v_ref[...], mk_ref[...]
    one = jnp.ones_like(values)
    sides = []
    for own in (low, jnp.logical_not(low)):
        sides.append((own, jnp.where(own, keys, mk), jnp.where(own, values, one)))
    count = q_ref.shape[0]
    block = min(ROWS, count)
    for start in range(0, count, block):
        rows = pl.ds(start, block)
        query, mq = q_ref[rows, :] * SCALE, mq_ref[rows, :]
        outs = []
        for own, some_keys, some_values in sides:
            scores = mm_nt(jnp.where(own, query, mq), some_keys)
            top = jnp.max(scores, axis=1, keepdims=True)
            expo = jnp.exp(scores - top).astype(bf16)
            mixed = mm(expo, some_values)
            total = pltpu.roll(mixed, DH, 1)
            outs.append((mixed / total, top + jnp.log(total)))
        attn_ref[rows, :] = jnp.where(low, outs[0][0], outs[1][0]).astype(bf16)
        lse_ref[rows, :] = jnp.where(low, outs[0][1], outs[1][1])


def three_parts(value):
    first = value.astype(bf16).astype(f32)
    rest = value - first
    second = rest.astype(bf16).astype(f32)
    return first, second, rest - second


def backward_heads(
    q_ref, k_ref, v_ref, mq_ref, mk_ref, attn_ref, lse_ref, grad_ref, dq_ref, dk_ref, dv_ref
):
    lane = lax.broadcasted_iota(jnp.int32, (1, PAIR), 1)
    place = lane % DH
    low = lane < DH
    query, mq, grad = q_ref[...] * SCALE, mq_ref[...], grad_ref[...]
    product = grad.astype(f32) * attn_ref[...].astype(f32)
    lse = three_parts(-pltpu.roll(lse_ref[...], DH, 1))
    count_keys = k_ref.shape[0]
    block = min(ROWS, count_keys)
    sides = []
    for own in (low, jnp.logical_not(low)):
        delta = three_parts(-jnp.sum(jnp.where(own, product, 0.0), axis=1, keepdims=True))
        more = jnp.where(place == 2, lse[0], jnp.where(place == 3, lse[1], lse[2]))
        more = jnp.where(place < 2, mq, jnp.where(place < 5, more, 0.0).astype(bf16))
        some_query = jnp.where(own, query, more)
        more = jnp.where(place == 0, delta[0], jnp.where(place == 1, delta[1], delta[2]))
        some_grad = jnp.where(own, grad, jnp.where(place < 3, more, 0.0).astype(bf16))
        sides.append((own, some_query, some_grad, None))
    totals = [None, None]
    for start in range(0, count_keys, block):
        rows = pl.ds(start, block)
        keys, values, mk = k_ref[rows, :], v_ref[rows, :], mk_ref[rows, :]
        ones = jnp.ones_like(values)
        zeros = jnp.zeros_like(values)
        more_keys = jnp.where(place < 2, mk, jnp.where(place < 5, ones, zeros))
        more_values = jnp.where(place < 3, ones, zeros)
        parts = []
        for side in range(2):
            own, some_query, some_grad, _ = sides[side]
            some_keys = jnp.where(own, keys, more_keys)
            some_values = jnp.where(own, values, more_values)
            probs = jnp.exp(mm_nt(some_keys, some_query))
            slope = (probs * mm_nt(some_values, some_grad)).astype(bf16)
            dv = mm(probs.astype(bf16), some_grad)
            dk = mm(slope, some_query)
            dq = mm_tn(slope, some_keys)
            totals[side] = dq if totals[side] is None else totals[side] + dq
            parts.append((dk, dv))
        dk_ref[rows, :] = jnp.where(low, parts[0][0], parts[1][0]).astype(bf16)
        dv_ref[rows, :] = jnp.where(low, parts[0][1], parts[1][1]).astype(bf16)
    dq_ref[...] = (jnp.where(low, totals[0], totals[1]) * SCALE).astype(bf16)


def head_block(rows, offset):
    return pl.BlockSpec((rows, PAIR), lambda i: (0, i + offset))


def fixed_block(rows):
    return pl.BlockSpec((rows, PAIR), lambda i: (0, 0))


def attention_forward(query_array, key_array, offsets, mq, mk):
    count, keys = query_array.shape[0], key_array.shape[0]
    pairs = H * DH // PAIR
    return pl.pallas_call(
        forward_heads,
        grid=(pairs,),
        out_shape=(
            jax.ShapeDtypeStruct((count, D), bf16),
            jax.ShapeDtypeStruct((count, D), f32),
        ),
        in_specs=[
            head_block(count, 0),
            head_block(keys, offsets[0]),
            head_block(keys, offsets[1]),
            fixed_block(count),
            fixed_block(keys),
        ],
        out_specs=(head_block(count, 0), head_block(count, 0)),
        cost_estimate=pl.CostEstimate(
            flops=16 * count * keys * D, bytes_accessed=8 * (count + keys) * D, transcendentals=count * keys * H
        ),
        name="attention_forward",
    )(query_array, key_array, key_array, mq, mk)


def attention_backward(query_array, key_array, offsets, mq, mk, attn, lse, grad):
    count, keys = query_array.shape[0], key_array.shape[0]
    pairs = H * DH // PAIR
    return pl.pallas_call(
        backward_heads,
        grid=(pairs,),
        out_shape=(
            jax.ShapeDtypeStruct((count, D), bf16),
            jax.ShapeDtypeStruct((keys, D), bf16),
            jax.ShapeDtypeStruct((keys, D), bf16),
        ),
        in_specs=[
            head_block(count, 0),
            head_block(keys, offsets[0]),
            head_block(keys, offsets[1]),
            fixed_block(count),
            fixed_block(keys),
            head_block(count, 0),
            head_block(count, 0),
            head_block(count, 0),
        ],
        out_specs=(head_block(count, 0), head_block(keys, 0), head_block(keys, 0)),
        cost_estimate=pl.CostEstimate(
            flops=40 * count * keys * D, bytes_accessed=16 * (count + keys) * D, transcendentals=count * keys * H
        ),
        name="attention_backward",
    )(query_array, key_array, key_array, mq, mk, attn, lse, grad)


def normalize(rows):
    mean = jnp.mean(rows, axis=-1, keepdims=True)
    centered = rows - mean
    inverse = lax.rsqrt(jnp.mean(centered * centered, axis=-1, keepdims=True) + EPS)
    return centered * inverse, inverse


def norm_back(grad, normed, inverse, gain):
    scaled = grad * gain
    first = jnp.mean(scaled, axis=-1, keepdims=True)
    second = jnp.mean(scaled * normed, axis=-1, keepdims=True)
    return inverse * (scaled - first - normed * second)


def swap(value, axis, size, move):
    return lax.ppermute(value, axis, [(i, move(i)) for i in range(size)])


def put(buffer, value, index, axis=0):
    return lax.dynamic_update_slice_in_dim(buffer, value, index * value.shape[axis], axis)


def pick(value, index, parts, axis=0):
    size = value.shape[axis] // parts
    return lax.dynamic_slice_in_dim(value, index * size, size, axis)


class Places:
    def __init__(self):
        self.reps = lax.axis_size("rep")
        self.shards = lax.axis_size("shard")
        self.rep = lax.axis_index("rep")
        self.shard = lax.axis_index("shard")
        self.core = self.rep % 2


def gather_rows(at, own):
    half = own.shape[0] // 2
    out = jnp.zeros((at.shards * own.shape[0],) + own.shape[1:], own.dtype)
    out = put(out, own, at.shard)
    mine = pick(own, at.core, 2)
    for step in range(1, at.shards):
        there = swap(mine, "shard", at.shards, lambda i: (i + at.shards - step) % at.shards)
        other = swap(there, "rep", at.reps, lambda i: i ^ 1)
        block = (at.shard + step) % at.shards * 2
        out = put(out, there, block + at.core)
        out = put(out, other, block + 1 - at.core)
    return out


def reduce_rows(at, grad):
    shards, columns = at.shards, grad.shape[1]
    rows = grad.shape[0] // shards
    value = grad.reshape(shards * 2, rows // 2, columns)
    value = grad.reshape(shards, 2, rows // 2, columns)
    mine = lax.dynamic_index_in_dim(value, at.core, 1, False)
    away = lax.dynamic_index_in_dim(value, 1 - at.core, 1, False).astype(bf16)
    value = mine.astype(f32) + swap(away, "rep", at.reps, lambda i: i ^ 1).astype(f32)
    total = lax.dynamic_index_in_dim(value, at.shard, 0, False)
    for step in range(1, shards):
        away = lax.dynamic_index_in_dim(value, (at.shard + step) % shards, 0, False).astype(bf16)
        total = total + swap(away, "shard", shards, lambda i: (i + step) % shards).astype(f32)
    stages = []
    bit = 2
    while bit < at.reps:
        axis = 0 if total.shape[0] % 32 == 0 else 1
        stages.append((bit, axis))
        up = (at.rep // bit) % 2
        mine, away = pick(total, up, 2, axis), pick(total, 1 - up, 2, axis).astype(bf16)
        move = functools.partial(lambda b, i: i ^ b, bit)
        total = mine + swap(away, "rep", at.reps, move).astype(f32)
        bit *= 2
    total = total.astype(bf16)
    for bit, axis in reversed(stages):
        up = (at.rep // bit) % 2
        move = functools.partial(lambda b, i: i ^ b, bit)
        other = swap(total, "rep", at.reps, move)
        shape = list(total.shape)
        shape[axis] *= 2
        both = jnp.zeros(shape, bf16)
        total = put(put(both, total, up, axis), other, 1 - up, axis)
    other = swap(total, "rep", at.reps, lambda i: i ^ 1)
    first = jnp.where(at.core == 0, total, other)
    second = jnp.where(at.core == 0, other, total)
    return jnp.concatenate([first, second], axis=0).astype(f32)


def spread(at, value):
    micro, shards = value.shape[0], at.shards
    parts = []
    for step in range(micro):
        moves = [(i, (i + step) % micro * (shards // micro) + i // micro) for i in range(shards)]
        part = lax.dynamic_index_in_dim(value, (at.shard + step) % micro, 0, False)
        if any(a != b for a, b in moves):
            part = lax.ppermute(part, "shard", moves)
        parts.append(part)
    return jnp.concatenate(parts, axis=0)


def collect(at, value, micro):
    shards = at.shards
    slots = value.shape[0] // micro
    out = jnp.zeros((micro, slots) + value.shape[1:], value.dtype)
    for step in range(micro):
        moves = [((i + step) % micro * (shards // micro) + i // micro, i) for i in range(shards)]
        part = value[step * slots : (step + 1) * slots]
        if any(a != b for a, b in moves):
            part = lax.ppermute(part, "shard", moves)
        out = lax.dynamic_update_index_in_dim(out, part, (at.shard + step) % micro, 0)
    return out


def rows_at(start, size):
    return pl.ds(pl.multiple_of(start, 16), size)


def cols_at(start, size):
    return pl.ds(pl.multiple_of(start, PAIR), size)


class Here:
    def __init__(self):
        self.rep = lax.axis_index("rep")
        self.y = lax.axis_index("shard")
        self.core = lax.rem(self.rep, 2)
        self.x = lax.rem(lax.div(self.rep, 2), 2)

    def across(self, bit):
        up = lax.rem(lax.div(self.rep, bit), 2)
        return {"rep": self.rep + bit * (1 - 2 * up)}

    def over(self):
        return {"shard": 1 - self.y}


class Copies:
    def __init__(self, send, recv):
        self.send, self.recv, self.used, self.open = send, recv, 0, []

    def away(self, source, target, peer):
        k = self.used
        self.used += 1
        copy = pltpu.make_async_remote_copy(
            src_ref=source,
            dst_ref=target,
            send_sem=self.send.at[k],
            recv_sem=self.recv.at[k],
            device_id=peer,
            device_id_type=pl.DeviceIdType.MESH,
        )
        return copy

    def near(self, source, target):
        k = self.used
        self.used += 1
        return pltpu.make_async_copy(source, target, self.recv.at[k])


def greet(peers):
    barrier = pltpu.get_barrier_semaphore()
    for peer in peers:
        pl.semaphore_signal(barrier, inc=1, device_id=peer, device_id_type=pl.DeviceIdType.MESH)
    pl.semaphore_wait(barrier, len(peers))


class Gathered:
    def __init__(self, here, copies, own, full, shard_rows, first_row, n, cols):
        h = n // 4
        q = 2 * here.x + here.core
        across = 2 * (1 - here.x) + here.core
        mine = here.y * shard_rows + first_row
        other = (1 - here.y) * shard_rows + first_row

        def at(start, size):
            return full.at[rows_at(start, size), cols]

        self.local = copies.near(own(0, n), at(mine, n))
        self.over = copies.away(own(q * h, h), at(mine + q * h, h), here.over())
        first, second = at(other + q * h, h), at(other + across * h, h)
        self.side = copies.away(first, first, here.across(2))
        self.core_one = copies.away(first, first, here.across(1))
        self.core_two = copies.away(second, second, here.across(1))

    def start(self):
        self.over.start()
        self.local.start()

    def forward_one(self):
        self.over.wait_recv()
        self.side.start()
        self.core_one.start()

    def forward_two(self):
        self.side.wait_recv()
        self.core_two.start()

    def ready(self):
        self.local.wait()
        self.core_one.wait_recv()
        self.core_two.wait_recv()

    def finish(self):
        for copy in (self.over, self.side, self.core_one, self.core_two):
            copy.wait_send()


def gelu_parts(pre):
    lower = 0.5 * (1.0 + lax.erf(pre * 0.7071067811865476))
    density = jnp.exp(-0.5 * pre * pre) * 0.3989422804014327
    return pre * lower, lower + pre * density


UNITS = 12


class Units:
    def __init__(self, here, reps, send, recv, swap_buffer, own, far, near, done, result):
        self.here, self.send, self.recv = here, send, recv
        self.swap_buffer, self.own, self.far, self.near, self.done = swap_buffer, own, far, near, done
        self.result = result
        self.n = own.shape[2]
        self.bits = []
        bit = 2
        while bit < reps:
            self.bits.append(bit)
            bit *= 2
        self.stages = 3 + 2 * len(self.bits)

    def copy(self, stage, u, source, target, peer):
        return pltpu.make_async_remote_copy(
            src_ref=source,
            dst_ref=target,
            send_sem=self.send.at[stage, u],
            recv_sem=self.recv.at[stage, u],
            device_id=peer,
            device_id_type=pl.DeviceIdType.MESH,
        )

    def slot(self, u, side):
        n = self.n
        return self.swap_buffer.at[rows_at(lax.rem(u, 4) * 2 * n, 2 * n), pl.ds(side * n, n)]

    def rows_of(self, level):
        size, start = self.n, 0
        for bit in self.bits[:level]:
            size //= 2
            start = start + lax.rem(lax.div(self.here.rep, bit), 2) * size
        return start, size

    def core_copy(self, u):
        return self.copy(0, u, self.slot(u, 0), self.slot(u, 1), self.here.across(1))

    def y_copy(self, u):
        return self.copy(1, u, self.own.at[u, 1 - self.here.y], self.far.at[u], self.here.over())

    def down_copy(self, k, u):
        start, size = self.rows_of(k)
        half = size // 2
        up = lax.rem(lax.div(self.here.rep, self.bits[k]), 2)
        rows = rows_at(start + (1 - up) * half, half)
        return self.copy(
            2 + k, u, self.own.at[u, self.here.y, rows, :], self.near[k].at[u], self.here.across(self.bits[k])
        )

    def up_copy(self, k, u):
        level = len(self.bits) - k
        start, size = self.rows_of(level)
        bit = self.bits[level - 1] if level else 1
        piece = self.done.at[u, self.here.core, rows_at(start, size), :]
        return self.copy(2 + len(self.bits) + k, u, piece, piece, self.here.across(bit))

    def out_copies(self, u):
        n = self.n
        down, up, *square = self.result
        for h in range(2):
            if u < 4:
                place = down.at[pl.ds(h * 2 * n + u // 2 * n, n), pl.ds(u % 2 * n, n)]
            elif u < 8:
                place = up.at[:, pl.ds(h * 4 * n + (u - 4) * n, n)]
            else:
                place = square[u - 8].at[:, pl.ds(h * n, n)]
            yield pltpu.make_async_copy(
                self.done.at[u, h], place, (self.send, self.recv)[h].at[self.stages, u]
            )

    def put_out(self, u):
        for copy in self.out_copies(u):
            copy.start()

    def first_sum(self, u):
        n, y = self.n, self.here.y
        self.core_copy(u).wait_recv()
        for shard in (1 - y, y):
            rows = rows_at((lax.rem(u, 4) * 2 + shard) * n, n)
            theirs = self.swap_buffer[rows, pl.ds(n, n)].astype(f32)
            self.own[u, shard] = (self.own[u, shard].astype(f32) + theirs).astype(bf16)
            if shard is not y:
                self.y_copy(u).start()

    def stage(self, k, u):
        bits = len(self.bits)
        y = self.here.y
        if k == 0:
            self.y_copy(u).wait_recv()
            start, size = self.rows_of(0)
            arrived = self.far
        elif k <= bits:
            self.down_copy(k - 1, u).wait_recv()
            arrived = self.near[k - 1]
            start, size = self.rows_of(k)
        if k < bits:
            half = size // 2
            up = lax.rem(lax.div(self.here.rep, self.bits[k]), 2)
            for part in (1 - up, up):
                rows = rows_at(start + part * half, half)
                theirs = arrived[u, rows_at(part * half, half), :].astype(f32)
                self.own[u, y, rows, :] = (self.own[u, y, rows, :].astype(f32) + theirs).astype(bf16)
                if part is not up:
                    self.down_copy(k, u).start()
        elif k == bits:
            rows = rows_at(start, size)
            total = self.own[u, y, rows, :].astype(f32) + arrived[u].astype(f32)
            self.done[u, self.here.core, rows, :] = total.astype(bf16)
            self.up_copy(0, u).start()
        else:
            self.up_copy(k - bits - 1, u).wait_recv()
            if k <= 2 * bits:
                self.up_copy(k - bits, u).start()
            elif isinstance(u, int):
                self.put_out(u)

    def tick(self, t):
        for k in reversed(range(2 * len(self.bits) + 2)):
            u = t - k
            if isinstance(u, int):
                if 0 <= u < UNITS:
                    self.stage(k, u)
            else:
                pl.when(jnp.logical_and(u >= 0, u < UNITS))(functools.partial(self.stage, k, u))

    def finish(self):
        @pl.loop(0, UNITS)
        def _(u):
            @pl.when(u >= UNITS - 4)
            def _():
                self.core_copy(u).wait_send()

            self.y_copy(u).wait_send()
            for k in range(len(self.bits)):
                self.down_copy(k, u).wait_send()
            for k in range(len(self.bits) + 1):
                self.up_copy(k, u).wait_send()

        for u in range(UNITS):
            for copy in self.out_copies(u):
                copy.wait()


def layer_kernel(
    tokens,
    cotangent,
    seq,
    *rest,
):
    lines, b_up, weights = rest[:8], rest[8], rest[9:15]
    layer_steps(tokens, cotangent, seq, lines, b_up, *weights, rest[15:24], *rest[24:])


def layer_steps(
    tokens,
    cotangent,
    seq,
    lines,
    b_up,
    w_query,
    w_key,
    w_value,
    w_attn,
    w_up,
    w_down,
    outs,
    x,
    slope,
    three,
    proj,
    up,
    down,
    raw_vectors,
    vecs,
    vec_up,
    qkv,
    heads,
    lse,
    mq,
    mk,
    normed,
    inverse,
    hidden,
    active,
    bend,
    branch,
    second,
    layer,
    sums,
    sums_up,
    others,
    own,
    far,
    near_x,
    near_z,
    near_w,
    done,
    small,
    send,
    recv,
    unit_send,
    unit_recv,
    free,
):
    reps = lax.axis_size("rep")
    here = Here()
    copies = Copies(send, recv)
    n = w_query.shape[0]
    y = here.y
    near = (near_x, near_z, near_w)
    o_layer, o_back, *o_grads, o_small = outs
    units = Units(here, reps, unit_send, unit_recv, down, own, far, near, done, o_grads)
    peers = [here.over(), here.across(1)] + [here.across(bit) for bit in units.bits]
    greet(peers)

    wide = up.shape[1] // (2 * n)

    def piece(weight, full, row, col, into):
        def own(start, size):
            return weight.at[rows_at(row + start, size), pl.ds(col, D)]

        return Gathered(here, copies, own, full, weight.shape[0], row, n, pl.ds(into + col, D))

    g_three = [piece(w, three, 0, 0, k * D) for k, w in enumerate((w_query, w_key, w_value))]
    g_attn = piece(w_attn, proj, 0, 0, 0)
    g_up = [piece(w_up, up, 0, k * D, 0) for k in range(up.shape[1] // D)]
    g_down = [piece(w_down, down, k * n, 0, 0) for k in range(w_down.shape[0] // n)]
    vec_away = copies.away(raw_vectors.at[y], raw_vectors.at[y], here.over())
    low, high = pl.ds(0, n), pl.ds(n, n)
    x_away = copies.away(tokens.at[1 - y], x.at[high, :], here.over())
    x_near = copies.near(tokens.at[y], x.at[low, :])
    s_away = copies.away(cotangent.at[1 - y], slope.at[high, :], here.over())
    s_near = copies.near(cotangent.at[y], slope.at[low, :])
    layer_away = copies.away(layer.at[high, :], o_layer.at[y], here.over())
    layer_near = copies.near(layer.at[low, :], o_layer.at[y])
    back_away = copies.away(hidden.at[high, :], o_back.at[y], here.over())
    back_near = copies.near(hidden.at[low, :], o_back.at[y])
    x_near.start()
    for part in g_three:
        part.start()
    for i, line in enumerate(lines):
        raw_vectors[y, i : i + 1, :] = line[...].astype(f32).reshape(1, n)
    for i in range(wide):
        raw_vectors[y, 8 + i : 9 + i, :] = b_up[i * n : (i + 1) * n].astype(f32).reshape(1, n)
    vec_away.start()
    x_away.start()
    for part in [g_attn] + g_up + g_down:
        part.start()
    s_away.start()
    s_near.start()

    length = seq[y, 0, 0]

    def inside(start, size):
        row = start + lax.broadcasted_iota(jnp.int32, (size, 1), 0)
        place = row + jnp.where(row < n, y * n, -y * n)
        return (place < length).astype(f32)

    first = inside(0, 2 * n)
    lane = lax.rem(lax.broadcasted_iota(jnp.int32, (1, PAIR), 1), DH)
    mq[...] = jnp.where(
        lane == 0, -BIG * first, jnp.where(lane == 1, -BIG * (1.0 - first), 0.0)
    ).astype(bf16)
    mk[...] = jnp.where(lane == 0, 1.0 - first, jnp.where(lane == 1, first, 0.0)).astype(bf16)
    sums[...] = jnp.zeros_like(sums)
    lse[...] = jnp.zeros_like(lse)

    for part in g_three:
        part.forward_one()
    for part in g_three:
        part.forward_two()
    vec_away.wait_recv()
    for half in range(2):
        table = raw_vectors[half]
        vecs[:, half * n : (half + 1) * n] = table
        for i in range(wide):
            start = half * wide * n + i * n
            vec_up[:, start : start + n] = table[8 + i : 9 + i, :]
    for part in g_three:
        part.ready()
    x_near.wait()
    tile = 256

    @pl.loop(0, 2)
    def _(half):
        pl.when(half == 1)(x_away.wait_recv)
        rows = rows_at(half * n, n)

        @pl.loop(0, 3 * D // tile)
        def _(i):
            cols = cols_at(i * tile, tile)
            which = lax.div(i, D // tile)
            inner = cols_at(lax.rem(i, D // tile) * tile, tile)
            bias = jnp.where(
                which == 0, vecs[0:1, inner], jnp.where(which == 2, vecs[1:2, inner], 0.0)
            )
            qkv[rows, cols] = (mm(x[rows, :], three[:, cols]) + bias).astype(bf16)

    lanes = lax.broadcasted_iota(jnp.int32, (1, PAIR), 1)
    left = lanes < DH
    pairs = H * DH // PAIR

    @pl.loop(0, pairs)
    def _(i):
        keys, values = qkv[:, cols_at(D + i * PAIR, PAIR)], qkv[:, cols_at(2 * D + i * PAIR, PAIR)]
        one = jnp.ones_like(values)
        sides = []
        for side in (left, jnp.logical_not(left)):
            sides.append((side, jnp.where(side, keys, mk[...]), jnp.where(side, values, one)))
        for start in range(0, 2 * n, ROWS):
            rows = pl.ds(start, ROWS)
            query = qkv[rows, cols_at(i * PAIR, PAIR)] * SCALE
            outs = []
            total_lse = lse[rows, :]
            for number, (side, some_keys, some_values) in enumerate(sides):
                scores = mm_nt(jnp.where(side, query, mq[rows, :]), some_keys)
                top = jnp.max(scores, axis=1, keepdims=True)
                expo = jnp.exp(scores - top).astype(bf16)
                mixed = mm(expo, some_values)
                total = pltpu.roll(mixed, DH, 1)
                outs.append(mixed / total)
                sum_all = jnp.where(side, total, mixed)
                total_lse = jnp.where(lanes == 2 * i + number, top + jnp.log(sum_all), total_lse)
            lse[rows, :] = total_lse
            heads[rows, cols_at(i * PAIR, PAIR)] = jnp.where(left, outs[0], outs[1]).astype(bf16)

        plan = [
            [g_attn.forward_one, g_up[0].forward_one, g_up[1].forward_one],
            [g_attn.forward_two, g_up[0].forward_two, g_up[2].forward_one],
            [g_up[1].forward_two, g_up[3].forward_one],
            [g_up[2].forward_two, g_down[0].forward_one],
            [g_up[3].forward_two, g_down[1].forward_one],
            [g_down[0].forward_two, g_down[2].forward_one],
        ]
        for number, steps in enumerate(plan):

            @pl.when(i == number)
            def _():
                for one in steps:
                    one()

    g_attn.ready()

    @pl.loop(0, 2 * n // ROWS)
    def _(i):
        rows = rows_at(i * ROWS, ROWS)
        resid = x[rows, :].astype(f32) + mm(heads[rows, :], proj[...]) + vecs[2:3, :]
        some, scale = normalize(resid)
        normed[rows, :] = some
        inverse[rows, :] = jnp.broadcast_to(scale, (ROWS, PAIR))
        hidden[rows, :] = (some * vecs[3:4, :] + vecs[4:5, :]).astype(bf16)

    g_down[1].forward_two()
    g_down[3].forward_one()
    for part in g_up:
        part.ready()

    @pl.loop(0, up.shape[1] // tile)
    def _(i):
        cols = cols_at(i * tile, tile)
        pre = mm(hidden[...], up[:, cols]) + vec_up[:, cols]
        value, rate = gelu_parts(pre)
        active[:, cols] = value.astype(bf16)
        bend[:, cols] = rate.astype(bf16)

        pl.when(i == 3)(g_down[2].forward_two)
        pl.when(i == 8)(g_down[3].forward_two)

    for part in g_down:
        part.ready()
    s_away.wait_recv()
    s_near.wait()

    @pl.loop(0, 2 * n // ROWS)
    def _(i):
        rows = rows_at(i * ROWS, ROWS)
        resid = mm(active[rows, :], down[...]) + vecs[5:6, :]
        resid = resid + (normed[rows, :] * vecs[3:4, :] + vecs[4:5, :])
        some, scale = normalize(resid)
        layer[rows, :] = (some * vecs[6:7, :] + vecs[7:8, :]).astype(bf16)
        grad = slope[rows, :].astype(f32) * inside(i * ROWS, ROWS)
        back = norm_back(grad, some, scale, vecs[6:7, :])
        low_back = back.astype(bf16)
        second[rows, :] = back
        branch[rows, :] = low_back
        sums[5:6, :] += jnp.sum(low_back.astype(f32), axis=0, keepdims=True)
        sums[6:7, :] += jnp.sum(grad * some, axis=0, keepdims=True)
        sums[7:8, :] += jnp.sum(grad, axis=0, keepdims=True)

    layer_away.start()
    layer_near.start()

    @pl.loop(0, up.shape[1] // tile)
    def _(i):
        cols = cols_at(i * tile, tile)
        rate = bend[:, cols].astype(f32)
        low_pre = (mm_nt(branch[...], down[rows_at(i * tile, tile), :]) * rate).astype(bf16)
        bend[:, cols] = low_pre
        sums_up[:, cols] = jnp.sum(low_pre.astype(f32), axis=0, keepdims=True)

    for part in g_down:
        part.finish()
    pl.semaphore_signal(
        free, inc=1, device_id=here.across(1), device_id_type=pl.DeviceIdType.MESH
    )
    c = here.core
    waited = False

    def make_pair(u, block):
        for one in (u, u + 1):
            if one >= 4:
                units.core_copy(one - 4).wait_send()
        for shard in range(2):
            value = block(shard, 1 - c)
            for k in range(2):
                rows = rows_at((u + k) % 4 * 2 * n + shard * n, n)
                down[rows, pl.ds(0, n)] = value[:, k * n : (k + 1) * n].astype(bf16)
        for one in (u - 2, u - 1):
            if one >= 0:
                units.first_sum(one)
        if u == 0:
            pl.semaphore_wait(free, 1)
        units.core_copy(u).start()
        units.core_copy(u + 1).start()
        for shard in range(2):
            value = block(shard, c)
            for k in range(2):
                own[u + k, shard] = value[:, k * n : (k + 1) * n].astype(bf16)

    def make_one(u, left_side, right_side, before):
        units.core_copy(u - 4).wait_send()
        for shard in range(2):
            value = mm_tn(left_side[:, shard * n : (shard + 1) * n], right_side)
            one, two = value[:, :n], value[:, n:]
            rows = pl.ds(u % 4 * 2 * n + shard * n, n)
            down[rows, pl.ds(0, n)] = jnp.where(c == 0, two, one).astype(bf16)
            own[u, shard] = jnp.where(c == 0, one, two).astype(bf16)
        for one in before:
            units.first_sum(one)
        units.core_copy(u).start()

    for r in range(2):
        make_pair(
            2 * r,
            lambda shard, h: mm_tn(
                active[:, cols_at(shard * 4 * n + h * 2 * n + r * n, n)], branch[...]
            ),
        )
    for p in range(2):
        make_pair(
            4 + 2 * p,
            lambda shard, h: mm_tn(
                hidden[:, shard * n : (shard + 1) * n], bend[:, cols_at(h * 4 * n + p * 2 * n, 2 * n)]
            ),
        )
        units.tick(p)

    @pl.loop(0, 2 * n // ROWS)
    def _(i):
        rows = rows_at(i * ROWS, ROWS)
        grad = mm_nt(bend[rows, :], up[...]) + second[rows, :]
        some = normed[rows, :]
        sums[3:4, :] += jnp.sum(grad * some, axis=0, keepdims=True)
        sums[4:5, :] += jnp.sum(grad, axis=0, keepdims=True)
        back = norm_back(grad, some, inverse[rows, 0:1], vecs[3:4, :])
        low_back = back.astype(bf16)
        second[rows, :] = back
        branch[rows, :] = low_back
        sums[2:3, :] += jnp.sum(low_back.astype(f32), axis=0, keepdims=True)
        slope[rows, :] = mm_nt(low_back, proj[...]).astype(bf16)

        @pl.when(i == 0)
        def _():
            units.first_sum(6)
            units.first_sum(7)

    units.tick(2)
    make_one(8, heads, branch[...], ())
    units.tick(3)
    place = lax.rem(lanes, DH)

    @pl.loop(0, pairs)
    def _(i):
        cols, key_cols, value_cols = [cols_at(part * D + i * PAIR, PAIR) for part in range(3)]
        query = qkv[:, cols] * SCALE
        grad = slope[:, cols]
        product = grad.astype(f32) * heads[:, cols].astype(f32)
        sides = []
        for number, side in enumerate((left, jnp.logical_not(left))):
            delta = three_parts(-jnp.sum(jnp.where(side, product, 0.0), axis=1, keepdims=True))
            logs = jnp.where(lanes == 2 * i + number, lse[...], 0.0)
            logs = three_parts(-jnp.sum(logs, axis=1, keepdims=True))
            more = jnp.where(place == 2, logs[0], jnp.where(place == 3, logs[1], logs[2]))
            more = jnp.where(place < 2, mq[...], jnp.where(place < 5, more, 0.0).astype(bf16))
            some_query = jnp.where(side, query, more)
            more = jnp.where(place == 0, delta[0], jnp.where(place == 1, delta[1], delta[2]))
            some_grad = jnp.where(side, grad, jnp.where(place < 3, more, 0.0).astype(bf16))
            sides.append((side, some_query, some_grad))
        totals = [None, None]
        for start in range(0, 2 * n, ROWS):
            rows = pl.ds(start, ROWS)
            keys, values = qkv[rows, key_cols], qkv[rows, value_cols]
            ones, zeros = jnp.ones_like(values), jnp.zeros_like(values)
            more_keys = jnp.where(place < 2, mk[rows, :], jnp.where(place < 5, ones, zeros))
            more_values = jnp.where(place < 3, ones, zeros)
            parts = []
            for number, (side, some_query, some_grad) in enumerate(sides):
                some_keys = jnp.where(side, keys, more_keys)
                some_values = jnp.where(side, values, more_values)
                probs = jnp.exp(mm_nt(some_keys, some_query))
                rate = (probs * mm_nt(some_values, some_grad)).astype(bf16)
                dv = mm(probs.astype(bf16), some_grad)
                dk = mm(rate, some_query)
                dq = mm_tn(rate, some_keys)
                totals[number] = dq if totals[number] is None else totals[number] + dq
                parts.append((dk, dv))
            active[rows, key_cols] = jnp.where(left, parts[0][0], parts[1][0]).astype(bf16)
            active[rows, value_cols] = jnp.where(left, parts[0][1], parts[1][1]).astype(bf16)
        active[:, cols] = (jnp.where(left, totals[0], totals[1]) * SCALE).astype(bf16)

        @pl.when(i == 0)
        def _():
            units.first_sum(8)

        @pl.when(i > 0)
        def _():
            units.tick(3 + i)

    for k in range(3):
        make_one(9 + k, x, active[:, k * D : (k + 1) * D], (8 + k,) if k else ())
        if k == 1:
            for u in range(2 * len(units.bits) + 1, 9):
                units.put_out(u - 2 * len(units.bits) - 1)
            units.tick(9)
    units.first_sum(11)
    sums[0:1, :] = jnp.sum(active[:, 0:D].astype(f32), axis=0, keepdims=True)
    sums[1:2, :] = jnp.sum(active[:, 2 * D : 3 * D].astype(f32), axis=0, keepdims=True)
    for i in range(up.shape[1] // D):
        sums[8 + i : 9 + i, :] = sums_up[:, i * D : (i + 1) * D]

    rounds = []
    ways = [here.across(1), here.over()] + [here.across(bit) for bit in units.bits]
    for k, way in enumerate(ways):
        rounds.append(copies.away(sums, others.at[k], way))
    rounds[0].start()

    @pl.loop(0, 2 * n // ROWS)
    def _(i):
        rows = rows_at(i * ROWS, ROWS)
        back = second[rows, :] + mm_nt(active[rows, 0 : 3 * D], three[...])
        hidden[rows, :] = back.astype(bf16)

    back_away.start()
    back_near.start()
    units.tick(10)
    last = UNITS + 2 * len(units.bits) + 1
    step = 0
    for t in range(11, last):
        units.tick(t)
        if step < len(rounds):
            rounds[step].wait()
            sums[...] += others[step]
            step += 1
            if step < len(rounds):
                rounds[step].start()
    while step < len(rounds):
        rounds[step].wait()
        sums[...] += others[step]
        step += 1
        if step < len(rounds):
            rounds[step].start()
    small[0:8, :] = sums[0:8, cols_at(y * n, n)]
    for i in range(wide):
        k = i * n // D
        from_row = 8 + wide // 2 * y + k
        small[8 + i : 9 + i, :] = sums[pl.ds(from_row, 1), i * n % D : i * n % D + n]
    small_out = copies.near(small, o_small)
    small_out.start()
    units.finish()
    small_out.wait()
    for copy in (layer_away, back_away):
        copy.wait()
    for copy in (layer_near, back_near):
        copy.wait()
    for part in g_three + [g_attn] + g_up:
        part.finish()
    for copy in (vec_away, x_away, s_away):
        copy.wait_send()


def run_layer(tokens, cotangent, seq, lines, b_up, weights, reps):
    n = weights[0].shape[0]
    count, wide = 2 * n, weights[4].shape[1]
    bits = reps.bit_length() - 2
    kinds = [
        ((2, n, D), bf16),
        ((2, n, D), bf16),
        ((4 * n, D), bf16),
        ((n, wide), bf16),
        ((n, D), bf16),
        ((n, D), bf16),
        ((n, D), bf16),
        ((n, D), bf16),
        ((16, n), f32),
    ]
    near = [((UNITS, max(16, n >> (k + 1)), n), bf16) for k in range(3)]
    scratch = [
        ((count, D), bf16),
        ((count, D), bf16),
        ((D, 3 * D), bf16),
        ((D, D), bf16),
        ((D, wide), bf16),
        ((wide, D), bf16),
        ((2, 16, n), f32),
        ((16, D), f32),
        ((1, wide), f32),
        ((count, 3 * D), bf16),
        ((count, D), bf16),
        ((count, PAIR), f32),
        ((count, PAIR), bf16),
        ((count, PAIR), bf16),
        ((count, D), f32),
        ((count, PAIR), f32),
        ((count, D), bf16),
        ((count, wide), bf16),
        ((count, wide), bf16),
        ((count, D), bf16),
        ((count, D), f32),
        ((count, D), bf16),
        ((16, D), f32),
        ((1, wide), f32),
        ((bits + 2, 16, D), f32),
        ((UNITS, 2, n, n), bf16),
        ((UNITS, n, n), bf16),
        *near,
        ((UNITS, 2, n, n), bf16),
        ((16, n), f32),
    ]
    anywhere = pl.BlockSpec(memory_space=pl.ANY)
    stages = 4 + 2 * bits
    return pl.pallas_call(
        layer_kernel,
        out_shape=[jax.ShapeDtypeStruct(*kind) for kind in kinds],
        in_specs=[anywhere, anywhere, pl.BlockSpec(memory_space=pltpu.SMEM)]
        + [pl.BlockSpec(memory_space=pltpu.VMEM)] * 9
        + [anywhere] * 6,
        out_specs=[anywhere] * len(kinds),
        scratch_shapes=[pltpu.VMEM(*kind) for kind in scratch]
        + [
            pltpu.SemaphoreType.DMA((80,)),
            pltpu.SemaphoreType.DMA((80,)),
            pltpu.SemaphoreType.DMA((stages, UNITS)),
            pltpu.SemaphoreType.DMA((stages, UNITS)),
            pltpu.SemaphoreType.REGULAR,
        ],
        compiler_params=pltpu.CompilerParams(
            collective_id=0, has_side_effects=True, vmem_limit_bytes=67043328
        ),
        name="encoder_layer",
    )(tokens, cotangent, seq, *lines, b_up, *weights)


def split_vectors(table, *outs):
    *lines, b_up = outs
    n = table.shape[1]
    for i, line in enumerate(lines):
        line[...] = table[i : i + 1, :].reshape(n)
    for i in range(b_up.shape[0] // n):
        b_up[pl.ds(i * n, n)] = table[8 + i : 9 + i, :].reshape(n)


def run_split(table, wide):
    n = table.shape[1]
    inside = pl.BlockSpec(memory_space=pltpu.VMEM)
    return pl.pallas_call(
        split_vectors,
        out_shape=[jax.ShapeDtypeStruct((n,), f32)] * 8 + [jax.ShapeDtypeStruct((wide * n,), f32)],
        in_specs=[inside],
        out_specs=[inside] * 9,
        name="split_vectors",
    )(table)


def general_body(
    tokens,
    cotangent,
    seq_lengths,
    w_query,
    b_query,
    w_key,
    w_value,
    b_value,
    w_attn,
    b_attn,
    norm_gain,
    norm_bias,
    w_up,
    b_up,
    w_down,
    b_down,
    out_gain,
    out_bias,
):
    at = Places()
    shards = at.shards
    micro, slots = tokens.shape[0], tokens.shape[1]
    span = shards // micro
    count = micro * slots
    x = spread(at, tokens)
    w_three = gather_rows(at, jnp.concatenate([w_query, w_key, w_value], axis=1))
    part = w_query.shape[0]
    wide = b_up.shape[0] // part
    vectors = jnp.concatenate(
        [
            jnp.stack(
                [b_query, b_value, b_attn, norm_gain, norm_bias, b_down, out_gain, out_bias]
            ),
            b_up.reshape(wide, part),
            jnp.zeros((16 - 8 - wide, part), bf16),
        ],
        axis=0,
    )
    table = put(jnp.zeros((shards,) + vectors.shape, bf16), vectors[None], at.shard)
    for step in range(1, shards):
        there = swap(vectors, "shard", shards, lambda i: (i + shards - step) % shards)
        table = put(table, there[None], (at.shard + step) % shards)
    table = table.astype(f32)
    (c_query, c_value, c_attn, c_gain, c_bias, c_down, c_out_gain, c_out_bias) = [
        table[:, i].reshape(1, D) for i in range(8)
    ]
    c_up = table[:, 8 : 8 + wide].reshape(1, D * wide)
    w_proj = gather_rows(at, w_attn)
    full_up = gather_rows(at, w_up)
    full_down = gather_rows(at, w_down)
    slope_in = spread(at, cotangent)

    group = slots * shards
    which, inner = at.shard // span, at.shard % span
    row = lax.dynamic_index_in_dim(seq_lengths[:, 0], which, 0, False)
    ids = segment_ids(row, group)

    def ids_of(device):
        parts = []
        for step in range(micro):
            source = micro * device + (which + micro - step) % micro
            parts.append(lax.dynamic_slice_in_dim(ids, source * slots, slots))
        return jnp.concatenate(parts)

    query_ids = ids_of(inner)
    nseq = seq_lengths.shape[-1] - 1
    valid = (query_ids < nseq).astype(f32)[:, None]
    three = mm(x, w_three) + jnp.concatenate([c_query, jnp.zeros_like(c_query), c_value], axis=1)
    three = three.astype(bf16)
    base = D // PAIR
    offsets = (base, 2 * base)
    key_array = three
    key_ids = [query_ids]
    if span > 1:
        offsets = (0, base)
        own = three[:, D:]
        parts = [own]
        for step in range(1, span):
            moves = [(i, i // span * span + (i + span - step) % span) for i in range(shards)]
            parts.append(lax.ppermute(own, "shard", moves))
            key_ids.append(ids_of((inner + step) % span))
        key_array = jnp.concatenate(parts, axis=0)
    mq, _ = mask_columns(query_ids)
    _, mk = mask_columns(jnp.concatenate(key_ids))
    attn, lse = attention_forward(three, key_array, offsets, mq, mk)

    normed_one, inverse_one = normalize(x.astype(f32) + mm(attn, w_proj) + c_attn)
    hidden = normed_one * c_gain + c_bias
    hidden_low = hidden.astype(bf16)
    pre = mm(hidden_low, full_up) + c_up
    lower = 0.5 * (1.0 + lax.erf(pre * 0.7071067811865476))
    active = (pre * lower).astype(bf16)
    density = jnp.exp(-0.5 * pre * pre) * 0.3989422804014327
    gelu_slope = lower + pre * density
    normed_two, inverse_two = normalize(hidden + mm(active, full_down) + c_down)
    layer = (normed_two * c_out_gain + c_out_bias).astype(bf16)
    grad_out = slope_in.astype(f32) * valid
    d_out_gain = jnp.sum(grad_out * normed_two, axis=0)
    d_out_bias = jnp.sum(grad_out, axis=0)
    grad_second = norm_back(grad_out, normed_two, inverse_two, c_out_gain)
    grad_branch = grad_second.astype(bf16)
    d_down = jnp.sum(grad_branch.astype(f32), axis=0)
    g_down = mm_tn(active, grad_branch)
    grad_pre = (mm_nt(grad_branch, full_down) * gelu_slope).astype(bf16)
    d_up = jnp.sum(grad_pre.astype(f32), axis=0)
    g_up = mm_tn(hidden_low, grad_pre)
    grad_hidden = mm_nt(grad_pre, full_up) + grad_second
    d_gain = jnp.sum(grad_hidden * normed_one, axis=0)
    d_bias = jnp.sum(grad_hidden, axis=0)
    grad_first = norm_back(grad_hidden, normed_one, inverse_one, c_gain)
    grad_proj = grad_first.astype(bf16)
    d_attn = jnp.sum(grad_proj.astype(f32), axis=0)
    g_attn = mm_tn(attn, grad_proj)
    grad_attn = mm_nt(grad_proj, w_proj).astype(bf16)
    dq, dk, dv = attention_backward(three, key_array, offsets, mq, mk, attn, lse, grad_attn)
    if span > 1:
        both = jnp.concatenate([dk, dv], axis=1)
        total = both[:count].astype(f32)
        for step in range(1, span):
            moves = [(i, i // span * span + (i + step) % span) for i in range(shards)]
            away = both[step * count : (step + 1) * count]
            total = total + lax.ppermute(away, "shard", moves).astype(f32)
        dk, dv = total[:, :D].astype(bf16), total[:, D:].astype(bf16)
    d_three = jnp.concatenate([dq, dk, dv], axis=1)
    d_query = jnp.sum(dq.astype(f32), axis=0)
    d_value = jnp.sum(dv.astype(f32), axis=0)
    g_three = mm_tn(x, d_three)
    back = (grad_first + mm_nt(d_three, w_three)).astype(bf16)

    sums = jnp.concatenate(
        [
            jnp.stack([d_query, d_value, d_attn, d_gain, d_bias, d_down, d_out_gain, d_out_bias]).reshape(
                8, shards, part
            ),
            d_up.reshape(shards, wide, part).transpose(1, 0, 2),
            jnp.zeros((PAIR - 8 - wide, shards, part), f32),
        ],
        axis=0,
    )
    sums = sums.reshape(PAIR, D).T
    r_down = reduce_rows(at, g_down)
    r_up = reduce_rows(at, g_up)
    r_attn = reduce_rows(at, g_attn)
    r_three = reduce_rows(at, jnp.concatenate([g_three, sums], axis=1))
    small = r_three[:, 3 * D :].T
    return (
        collect(at, layer, micro),
        collect(at, back, micro),
        r_three[:, :D],
        small[0],
        r_three[:, D : 2 * D],
        r_three[:, 2 * D : 3 * D],
        small[1],
        r_attn,
        small[2],
        small[3],
        small[4],
        r_up,
        small[8 : 8 + wide].reshape(wide * part),
        r_down,
        small[5],
        small[6],
        small[7],
    )


def body(tokens, cotangent, seq_lengths, *weights):
    shards, micro = lax.axis_size("shard"), tokens.shape[0]
    reps = lax.axis_size("rep")
    if shards != 2 or micro != 2 or reps not in (4, 8, 16):
        return general_body(tokens, cotangent, seq_lengths, *weights)
    (
        w_query,
        b_query,
        w_key,
        w_value,
        b_value,
        w_attn,
        b_attn,
        norm_gain,
        norm_bias,
        w_up,
        b_up,
        w_down,
        b_down,
        out_gain,
        out_bias,
    ) = weights
    part = w_query.shape[0]
    wide = b_up.shape[0] // part
    lines = [b_query, b_value, b_attn, norm_gain, norm_bias, b_down, out_gain, out_bias]
    layer, back, *grads, small = run_layer(
        tokens,
        cotangent,
        seq_lengths,
        lines,
        b_up,
        (w_query, w_key, w_value, w_attn, w_up, w_down),
        reps,
    )
    g_down, g_up, g_attn, g_query, g_key, g_value = [grad.astype(f32) for grad in grads]
    d_query, d_value, d_attn, d_gain, d_bias, d_down, d_out_gain, d_out_bias, d_up = run_split(small, wide)
    return (
        layer,
        back,
        g_query,
        d_query,
        g_key,
        g_value,
        d_value,
        g_attn,
        d_attn,
        d_gain,
        d_bias,
        g_up,
        d_up,
        g_down,
        d_down,
        d_out_gain,
        d_out_bias,
    )


def solution(mesh):
    rows, vector = P("shard", None), P("shard")
    tokens = P(None, ("rep", "shard"), None)
    weights = (rows, vector, rows, rows, vector, rows, vector, vector, vector)
    weights += (rows, vector, rows, vector, vector, vector)
    return jax.shard_map(
        body,
        mesh=mesh,
        in_specs=(tokens, tokens, P(None, "rep", None)) + weights,
        out_specs=(tokens, tokens) + weights,
        check_vma=False,
    )
```

profile of v0, /device:TPU:1, one launch (start us, length us, event | category | flops | bytes accessed | tf_op | source)
XLA Modules:
  0.0 235.1 jit_solution(14885462793470325354)
XLA Ops:
  0.7 218.2 %encoder_layer.1 = (bf16[2,384,768]{2,1,0:T(8,128)(2,1)}, bf16[2,384,768]{2,1,0:T(8,128)(2,1)}, bf16[1536,768]{1,0:T(8,128)(2,1)}, bf16[384,3072]{1,0:T(8,128)(2...) custom-call(bf16[2,384,768]{2,1,0:T(8,128)(2,1)} %tokens.1, ...), custom_call_target="tpu_custom_call" | custom-call | tf_op jit(solution)/shard_map/encoder_layer/pallas_call | solution.py:1043
  218.8 1.4 split_vectors.1
  220.2 0.0 copy-start
  220.2 4.6 %convert_element_type.22 = f32[384,3072]{1,0:T(8,128)} convert(bf16[384,3072]{1,0:T(8,128)(2,1)} %get-tuple-element.47) | non-fusion elementwise | flops 1179648 | bytes 7077888 | tf_op jit(solution)/shard_map/convert_element_type | solution.py:1287
  224.8 0.0 copy-done
  224.8 0.0 copy-start.6
  224.8 2.5 %convert_element_type.23 = f32[1536,768]{1,0:T(8,128)} convert(bf16[1536,768]{1,0:T(8,128)(2,1)S(1)} %copy-done) | non-fusion elementwise | flops 1179648 | bytes 7077888 | tf_op jit(solution)/shard_map/convert_element_type | solution.py:1287
  227.3 0.0 copy-start.5
  227.3 0.0 copy-done.6
  227.3 1.1 convert_element_type.18
  228.4 0.0 copy-start.4
  228.4 0.2 copy-done.5
  228.6 1.1 convert_element_type.19
  229.7 0.0 copy-start.3
  229.7 0.0 copy-done.4
  229.7 1.1 convert_element_type.20
  230.8 0.0 copy-start.2
  230.8 0.2 copy-done.3
  230.9 1.1 convert_element_type.21
  232.0 0.3 copy-done.2
  232.3 0.0 copy-start.1
  232.3 1.0 copy.37
  233.4 0.7 copy-done.1
  234.0 1.0 copy.38
Async XLA Ops:
  220.2 4.6 %copy-start = (bf16[1536,768]{1,0:T(8,128)(2,1)S(1)}, bf16[1536,768]{1,0:T(8,128)(2,1)}, u32[]{:S(2)}) copy-start(bf16[1536,768]{1,0:T(8,128)(2,1)} %get-tuple-element.49) | copy-start | bytes 7077892
  224.8 2.6 %copy-start.6 = (bf16[384,768]{1,0:T(8,128)(2,1)S(1)}, bf16[384,768]{1,0:T(8,128)(2,1)}, u32[]{:S(2)}) copy-start(bf16[384,768]{1,0:T(8,128)(2,1)} %get-tuple-element.37) | copy-start | bytes 1769476
  227.3 1.3 copy-start.5
  228.4 1.3 copy-start.4
  229.7 1.3 copy-start.3
  230.8 1.6 copy-start.2
  232.3 1.7 copy-start.1
where the time goes:
time: 235 us
  Pallas kernels  220 us (94%)
  other arithmetic  11.5 us (5%)
  local copies, waits for them, and re-layouts  3.36 us (1%)
    pallas_call x1, Pallas kernels, run_layer(): pl.pallas_call(layer_kernel, out_shape=[jax.ShapeDtypeStruct(*kind) for k...  218 us
    convert_element_type x6, other arithmetic, body(): grad.astype(f32)  11.5 us

commit v1 on v0

--- a/solution.py
+++ b/solution.py
@@ -312,9 +312,11 @@
         self.core = lax.rem(self.rep, 2)
         self.x = lax.rem(lax.div(self.rep, 2), 2)
 
+    def up(self, bit):
+        return lax.rem(lax.div(self.rep, bit), 2)
+
     def across(self, bit):
-        up = lax.rem(lax.div(self.rep, bit), 2)
-        return {"rep": self.rep + bit * (1 - 2 * up)}
+        return {"rep": self.rep + bit * (1 - 2 * self.up(bit))}
 
     def over(self):
         return {"shard": 1 - self.y}
@@ -351,43 +353,44 @@
 
 
 class Gathered:
-    def __init__(self, here, copies, own, full, shard_rows, first_row, n, cols):
-        h = n // 4
-        q = 2 * here.x + here.core
-        across = 2 * (1 - here.x) + here.core
-        mine = here.y * shard_rows + first_row
-        other = (1 - here.y) * shard_rows + first_row
-
+    def __init__(self, here, copies, own, full, mine, other, n, cols, bits):
         def at(start, size):
             return full.at[rows_at(start, size), cols]
 
+        def held(level):
+            start, size = here.core * (n // 2), n // 2
+            for bit in reversed(bits[level:]):
+                size //= 2
+                start = start + here.up(bit) * size
+            return start, size
+
+        start, size = held(0)
         self.local = copies.near(own(0, n), at(mine, n))
-        self.over = copies.away(own(q * h, h), at(mine + q * h, h), here.over())
-        first, second = at(other + q * h, h), at(other + across * h, h)
-        self.side = copies.away(first, first, here.across(2))
-        self.core_one = copies.away(first, first, here.across(1))
-        self.core_two = copies.away(second, second, here.across(1))
+        self.hops = [copies.away(own(start, size), at(mine + start, size), here.over())]
+        for level, bit in enumerate(list(bits) + [1]):
+            start, size = held(level)
+            part = at(other + start, size)
+            self.hops.append(copies.away(part, part, here.across(bit)))
+        self.progress = 0
 
     def start(self):
-        self.over.start()
+        self.hops[0].start()
         self.local.start()
 
-    def forward_one(self):
-        self.over.wait_recv()
-        self.side.start()
-        self.core_one.start()
-
-    def forward_two(self):
-        self.side.wait_recv()
-        self.core_two.start()
+    def step(self):
+        if self.progress + 1 < len(self.hops):
+            self.hops[self.progress].wait_recv()
+            self.progress += 1
+            self.hops[self.progress].start()
 
     def ready(self):
+        while self.progress + 1 < len(self.hops):
+            self.step()
         self.local.wait()
-        self.core_one.wait_recv()
-        self.core_two.wait_recv()
+        self.hops[-1].wait_recv()
 
     def finish(self):
-        for copy in (self.over, self.side, self.core_one, self.core_two):
+        for copy in self.hops:
             copy.wait_send()
 
 
@@ -398,6 +401,44 @@
 
 
 UNITS = 12
+WAYS = (1, 0, 1, 0, 1, 2, 1, 0, 0, 0, 0, 0)
+PLAN = (
+    (3, 4),
+    (5, 3, 6, 4),
+    (7, 5, 8),
+    (9, 3, 4, 10, 6),
+    (7, 11, 9, 5),
+    (8, 6, 10),
+    (11, 7),
+    (8,),
+    (9, 10),
+    (11,),
+    (),
+    (),
+    (),
+    (),
+    (22, 23),
+    (21, 20),
+    (22, 25),
+    (21, 24, 20),
+    (22, 23),
+    (27, 21, 20, 25),
+    (22, 23, 26, 24, 21, 27),
+    (20, 25, 22, 28, 23),
+    (24, 21, 26, 27, 28),
+    (20, 25, 22, 21),
+    (21, 23, 24, 20, 26),
+    (20,),
+    (27, 22, 28),
+    (25, 23, 22),
+    (24, 25, 40, 26),
+    (29, 27),
+    (23, 28),
+    (24, 23, 29, 25, 30, 25, 26, 24, 27, 24, 28, 30, 29, 31, 26, 40, 27, 28, 27, 30, 31, 29, 26, 30, 31, 40, 26, 29, 28, 30, 28, 31, 40, 29, 30, 31, 29, 40, 29, 31, 30, 30, 31, 31),
+    (),
+    (),
+    (20, 21),
+)
 
 
 class Units:
@@ -405,13 +446,20 @@
         self.here, self.send, self.recv = here, send, recv
         self.swap_buffer, self.own, self.far, self.near, self.done = swap_buffer, own, far, near, done
         self.result = result
-        self.n = own.shape[2]
-        self.bits = []
+        self.n = own.shape[4]
+        self.all_bits = []
         bit = 2
         while bit < reps:
-            self.bits.append(bit)
+            self.all_bits.append(bit)
             bit *= 2
-        self.stages = 3 + 2 * len(self.bits)
+        self.progress = [0] * UNITS
+        self.stages = 3 + 2 * len(self.all_bits)
+
+    def bits(self, u):
+        bits = list(self.all_bits)
+        if WAYS[u] == 2 and len(bits) > 1:
+            bits[0], bits[1] = bits[1], bits[0]
+        return bits
 
     def copy(self, stage, u, source, target, peer):
         return pltpu.make_async_remote_copy(
@@ -425,120 +473,156 @@
 
     def slot(self, u, side):
         n = self.n
-        return self.swap_buffer.at[rows_at(lax.rem(u, 4) * 2 * n, 2 * n), pl.ds(side * n, n)]
-
-    def rows_of(self, level):
-        size, start = self.n, 0
-        for bit in self.bits[:level]:
-            size //= 2
-            start = start + lax.rem(lax.div(self.here.rep, bit), 2) * size
-        return start, size
+        if u < 4:
+            return (self.done, self.own)[side].at[UNITS - 4 + u]
+        return self.swap_buffer.at[pl.ds(u % 4 * 2 * n, 2 * n), pl.ds(side * n, n)]
+
+    def lay(self, u, shard, value):
+        n = self.n
+        if u < 4:
+            for part in range(2):
+                rows = value[part * (n // 2) : (part + 1) * (n // 2), :]
+                self.done[UNITS - 4 + u, shard, part] = rows.astype(bf16)
+        else:
+            rows = pl.ds(u % 4 * 2 * n + shard * n, n)
+            self.swap_buffer[rows, pl.ds(0, n)] = value.astype(bf16)
+
+    def theirs(self, u, shard, part):
+        n = self.n
+        if u < 4:
+            return self.own[UNITS - 4 + u, shard, part]
+        rows = rows_at(u % 4 * 2 * n + shard * n + part * (n // 2), n // 2)
+        return self.swap_buffer[rows, pl.ds(n, n)]
 
     def core_copy(self, u):
         return self.copy(0, u, self.slot(u, 0), self.slot(u, 1), self.here.across(1))
 
-    def y_copy(self, u):
-        return self.copy(1, u, self.own.at[u, 1 - self.here.y], self.far.at[u], self.here.over())
-
-    def down_copy(self, k, u):
-        start, size = self.rows_of(k)
+    def away_copy(self, k, u):
+        y, own, here = self.here.y, self.own, self.here
+        bits = self.bits(u)
+        up = here.up(bits[0])
+        first_y = WAYS[u] == 0
+        if k == 0 and first_y:
+            return self.copy(1, u, own.at[u, 1 - y], self.far.at[u], here.over())
+        if k == 0:
+            return self.copy(1, u, own.at[u, :, 1 - up], self.far.at[u], here.across(bits[0]))
+        if k == 1 and first_y:
+            return self.copy(2, u, own.at[u, y, 1 - up], self.near[0].at[u], here.across(bits[0]))
+        if k == 1:
+            return self.copy(2, u, own.at[u, 1 - y, up], self.near[0].at[u], here.over())
+        start, size = self.inner(u, k - 2)
         half = size // 2
-        up = lax.rem(lax.div(self.here.rep, self.bits[k]), 2)
-        rows = rows_at(start + (1 - up) * half, half)
+        rows = rows_at(start + (1 - here.up(bits[k - 1])) * half, half)
         return self.copy(
-            2 + k, u, self.own.at[u, self.here.y, rows, :], self.near[k].at[u], self.here.across(self.bits[k])
+            1 + k, u, own.at[u, y, up, rows, :], self.near[k - 1].at[u], here.across(bits[k - 1])
         )
 
-    def up_copy(self, k, u):
-        level = len(self.bits) - k
-        start, size = self.rows_of(level)
-        bit = self.bits[level - 1] if level else 1
-        piece = self.done.at[u, self.here.core, rows_at(start, size), :]
-        return self.copy(2 + len(self.bits) + k, u, piece, piece, self.here.across(bit))
+    def inner(self, u, level):
+        size, start = self.n // 2, 0
+        for bit in self.bits(u)[1 : 1 + level]:
+            size //= 2
+            start = start + self.here.up(bit) * size
+        return start, size
+
+    def back_copy(self, k, u):
+        bits = self.bits(u)
+        level = len(bits) - k
+        piece = self.done.at[u, self.here.core]
+        bit = bits[level - 1] if level else 1
+        if level:
+            start, size = self.inner(u, level - 1)
+            piece = self.done.at[u, self.here.core, self.here.up(bits[0]), rows_at(start, size), :]
+        return self.copy(2 + len(bits) + k, u, piece, piece, self.here.across(bit))
 
     def out_copies(self, u):
         n = self.n
         down, up, *square = self.result
         for h in range(2):
-            if u < 4:
-                place = down.at[pl.ds(h * 2 * n + u // 2 * n, n), pl.ds(u % 2 * n, n)]
-            elif u < 8:
-                place = up.at[:, pl.ds(h * 4 * n + (u - 4) * n, n)]
+            for part in range(2):
+                rows = part * (n // 2)
+                if u < 4:
+                    place = down.at[pl.ds(h * 2 * n + u // 2 * n + rows, n // 2), pl.ds(u % 2 * n, n)]
+                elif u < 8:
+                    place = up.at[pl.ds(rows, n // 2), pl.ds(h * 4 * n + (u - 4) * n, n)]
+                else:
+                    place = square[u - 8].at[pl.ds(rows, n // 2), pl.ds(h * n, n)]
+                yield pltpu.make_async_copy(
+                    self.done.at[u, h, part], place, (self.send, self.recv)[h].at[self.stages + part, u]
+                )
+
+    def keep(self, u, shard, value):
+        half = self.n // 2
+        for part in range(2):
+            self.own[u, shard, part] = value[part * half : (part + 1) * half, :].astype(bf16)
+
+    def first_sum(self, u):
+        y = self.here.y
+        up = self.here.up(self.bits(u)[0])
+        self.core_copy(u).wait_recv()
+        if WAYS[u] == 0:
+            order = [(1 - y, 0), (1 - y, 1), (y, 0), (y, 1)]
+        else:
+            order = [(0, 1 - up), (1, 1 - up), (0, up), (1, up)]
+        for number, (shard, part) in enumerate(order):
+            theirs = self.theirs(u, shard, part).astype(f32)
+            self.own[u, shard, part] = (self.own[u, shard, part].astype(f32) + theirs).astype(bf16)
+            if number == 1:
+                self.away_copy(0, u).start()
+
+    def step(self, u):
+        bits = len(self.all_bits)
+        k = self.progress[u]
+        if k > 2 * bits + 1:
+            return
+        self.progress[u] = k + 1
+        y, own = self.here.y, self.own
+        up = self.here.up(self.bits(u)[0])
+        if k <= bits:
+            self.away_copy(k, u).wait_recv()
+        if k == 0:
+            if WAYS[u] == 0:
+                order = [((y, 1 - up), 1 - up), ((y, up), up)]
             else:
-                place = square[u - 8].at[:, pl.ds(h * n, n)]
-            yield pltpu.make_async_copy(
-                self.done.at[u, h], place, (self.send, self.recv)[h].at[self.stages, u]
-            )
-
-    def put_out(self, u):
-        for copy in self.out_copies(u):
-            copy.start()
-
-    def first_sum(self, u):
-        n, y = self.n, self.here.y
-        self.core_copy(u).wait_recv()
-        for shard in (1 - y, y):
-            rows = rows_at((lax.rem(u, 4) * 2 + shard) * n, n)
-            theirs = self.swap_buffer[rows, pl.ds(n, n)].astype(f32)
-            self.own[u, shard] = (self.own[u, shard].astype(f32) + theirs).astype(bf16)
-            if shard is not y:
-                self.y_copy(u).start()
-
-    def stage(self, k, u):
-        bits = len(self.bits)
-        y = self.here.y
-        if k == 0:
-            self.y_copy(u).wait_recv()
-            start, size = self.rows_of(0)
-            arrived = self.far
-        elif k <= bits:
-            self.down_copy(k - 1, u).wait_recv()
-            arrived = self.near[k - 1]
-            start, size = self.rows_of(k)
-        if k < bits:
+                order = [((1 - y, up), 1 - y), ((y, up), y)]
+            for number, ((shard, part), source) in enumerate(order):
+                theirs = self.far[u, source].astype(f32)
+                own[u, shard, part] = (own[u, shard, part].astype(f32) + theirs).astype(bf16)
+                if number == 0:
+                    self.away_copy(1, u).start()
+        elif k < bits:
+            start, size = self.inner(u, k - 1)
             half = size // 2
-            up = lax.rem(lax.div(self.here.rep, self.bits[k]), 2)
-            for part in (1 - up, up):
+            side = self.here.up(self.bits(u)[k])
+            for number, part in enumerate((1 - side, side)):
                 rows = rows_at(start + part * half, half)
-                theirs = arrived[u, rows_at(part * half, half), :].astype(f32)
-                self.own[u, y, rows, :] = (self.own[u, y, rows, :].astype(f32) + theirs).astype(bf16)
-                if part is not up:
-                    self.down_copy(k, u).start()
+                theirs = self.near[k - 1][u, rows_at(part * half, half), :].astype(f32)
+                own[u, y, up, rows, :] = (own[u, y, up, rows, :].astype(f32) + theirs).astype(bf16)
+                if number == 0:
+                    self.away_copy(k + 1, u).start()
         elif k == bits:
-            rows = rows_at(start, size)
-            total = self.own[u, y, rows, :].astype(f32) + arrived[u].astype(f32)
-            self.done[u, self.here.core, rows, :] = total.astype(bf16)
-            self.up_copy(0, u).start()
+            start, size = self.inner(u, k - 1)
+            total = own[u, y, up, rows_at(start, size), :].astype(f32)
+            total = total + self.near[k - 1][u].astype(f32)
+            self.done[u, self.here.core, up, rows_at(start, size), :] = total.astype(bf16)
+            self.back_copy(0, u).start()
         else:
-            self.up_copy(k - bits - 1, u).wait_recv()
+            self.back_copy(k - bits - 1, u).wait_recv()
             if k <= 2 * bits:
-                self.up_copy(k - bits, u).start()
-            elif isinstance(u, int):
-                self.put_out(u)
-
-    def tick(self, t):
-        for k in reversed(range(2 * len(self.bits) + 2)):
-            u = t - k
-            if isinstance(u, int):
-                if 0 <= u < UNITS:
-                    self.stage(k, u)
+                self.back_copy(k - bits, u).start()
             else:
-                pl.when(jnp.logical_and(u >= 0, u < UNITS))(functools.partial(self.stage, k, u))
+                for copy in self.out_copies(u):
+                    copy.start()
 
     def finish(self):
-        @pl.loop(0, UNITS)
-        def _(u):
-            @pl.when(u >= UNITS - 4)
-            def _():
+        for u in range(UNITS):
+            while self.progress[u] <= 2 * len(self.all_bits) + 1:
+                self.step(u)
+        for u in range(UNITS):
+            if u >= UNITS - 4:
                 self.core_copy(u).wait_send()
-
-            self.y_copy(u).wait_send()
-            for k in range(len(self.bits)):
-                self.down_copy(k, u).wait_send()
-            for k in range(len(self.bits) + 1):
-                self.up_copy(k, u).wait_send()
-
-        for u in range(UNITS):
+            for k in range(len(self.all_bits) + 1):
+                self.away_copy(k, u).wait_send()
+                self.back_copy(k, u).wait_send()
             for copy in self.out_copies(u):
                 copy.wait()
 
@@ -612,16 +696,33 @@
     near = (near_x, near_z, near_w)
     o_layer, o_back, *o_grads, o_small = outs
     units = Units(here, reps, unit_send, unit_recv, down, own, far, near, done, o_grads)
-    peers = [here.over(), here.across(1)] + [here.across(bit) for bit in units.bits]
+    peers = [here.over(), here.across(1)] + [here.across(bit) for bit in units.all_bits]
     greet(peers)
 
     wide = up.shape[1] // (2 * n)
+
+    pieces = []
 
     def piece(weight, full, row, col, into):
         def own(start, size):
             return weight.at[rows_at(row + start, size), pl.ds(col, D)]
 
-        return Gathered(here, copies, own, full, weight.shape[0], row, n, pl.ds(into + col, D))
+        rows = weight.shape[0]
+        bits = units.all_bits[:2]
+        pieces.append(
+            Gathered(
+                here,
+                copies,
+                own,
+                full,
+                y * rows + row,
+                (1 - y) * rows + row,
+                n,
+                pl.ds(into + col, D),
+                bits if len(pieces) % 2 == 0 else bits[::-1],
+            )
+        )
+        return pieces[-1]
 
     g_three = [piece(w, three, 0, 0, k * D) for k, w in enumerate((w_query, w_key, w_value))]
     g_attn = piece(w_attn, proj, 0, 0, 0)
@@ -667,10 +768,9 @@
     sums[...] = jnp.zeros_like(sums)
     lse[...] = jnp.zeros_like(lse)
 
-    for part in g_three:
-        part.forward_one()
-    for part in g_three:
-        part.forward_two()
+    for _ in range(3):
+        for part in g_three:
+            part.step()
     vec_away.wait_recv()
     for half in range(2):
         table = raw_vectors[half]
@@ -698,6 +798,38 @@
             )
             qkv[rows, cols] = (mm(x[rows, :], three[:, cols]) + bias).astype(bf16)
 
+    rounds = []
+    ways = [here.across(1), here.over()] + [here.across(bit) for bit in units.all_bits]
+    for k, way in enumerate(ways):
+        rounds.append(copies.away(sums, others.at[k], way))
+    round_done = [0]
+
+    def next_round():
+        k = round_done[0]
+        if k < len(rounds):
+            round_done[0] = k + 1
+            rounds[k].wait()
+            sums[...] += others[k]
+            if k + 1 < len(rounds):
+                rounds[k + 1].start()
+
+    def visit(place):
+        for one in PLAN[place]:
+            if one == 40:
+                next_round()
+            elif one >= 20:
+                units.step(one - 20)
+            else:
+                pieces[one].step()
+
+    def visit_one_of(i, places):
+        for number, place in enumerate(places):
+
+            @pl.when(i == number)
+            def _():
+                visit(place)
+
+    visit(0)
     lanes = lax.broadcasted_iota(jnp.int32, (1, PAIR), 1)
     left = lanes < DH
     pairs = H * DH // PAIR
@@ -726,20 +858,7 @@
             lse[rows, :] = total_lse
             heads[rows, cols_at(i * PAIR, PAIR)] = jnp.where(left, outs[0], outs[1]).astype(bf16)
 
-        plan = [
-            [g_attn.forward_one, g_up[0].forward_one, g_up[1].forward_one],
-            [g_attn.forward_two, g_up[0].forward_two, g_up[2].forward_one],
-            [g_up[1].forward_two, g_up[3].forward_one],
-            [g_up[2].forward_two, g_down[0].forward_one],
-            [g_up[3].forward_two, g_down[1].forward_one],
-            [g_down[0].forward_two, g_down[2].forward_one],
-        ]
-        for number, steps in enumerate(plan):
-
-            @pl.when(i == number)
-            def _():
-                for one in steps:
-                    one()
+        visit_one_of(i, range(1, 7))
 
     g_attn.ready()
 
@@ -752,21 +871,19 @@
         inverse[rows, :] = jnp.broadcast_to(scale, (ROWS, PAIR))
         hidden[rows, :] = (some * vecs[3:4, :] + vecs[4:5, :]).astype(bf16)
 
-    g_down[1].forward_two()
-    g_down[3].forward_one()
-    for part in g_up:
+    visit(7)
+    for number, part in enumerate(g_up):
         part.ready()
 
-    @pl.loop(0, up.shape[1] // tile)
-    def _(i):
-        cols = cols_at(i * tile, tile)
-        pre = mm(hidden[...], up[:, cols]) + vec_up[:, cols]
-        value, rate = gelu_parts(pre)
-        active[:, cols] = value.astype(bf16)
-        bend[:, cols] = rate.astype(bf16)
-
-        pl.when(i == 3)(g_down[2].forward_two)
-        pl.when(i == 8)(g_down[3].forward_two)
+        @pl.loop(number * D // tile, (number + 1) * D // tile)
+        def _(i):
+            cols = cols_at(i * tile, tile)
+            pre = mm(hidden[...], up[:, cols]) + vec_up[:, cols]
+            value, rate = gelu_parts(pre)
+            active[:, cols] = value.astype(bf16)
+            bend[:, cols] = rate.astype(bf16)
+
+        visit(8 + number)
 
     for part in g_down:
         part.ready()
@@ -789,54 +906,34 @@
         sums[6:7, :] += jnp.sum(grad * some, axis=0, keepdims=True)
         sums[7:8, :] += jnp.sum(grad, axis=0, keepdims=True)
 
-    layer_away.start()
-    layer_near.start()
-
-    @pl.loop(0, up.shape[1] // tile)
-    def _(i):
-        cols = cols_at(i * tile, tile)
-        rate = bend[:, cols].astype(f32)
-        low_pre = (mm_nt(branch[...], down[rows_at(i * tile, tile), :]) * rate).astype(bf16)
-        bend[:, cols] = low_pre
-        sums_up[:, cols] = jnp.sum(low_pre.astype(f32), axis=0, keepdims=True)
-
-    for part in g_down:
-        part.finish()
-    pl.semaphore_signal(
-        free, inc=1, device_id=here.across(1), device_id_type=pl.DeviceIdType.MESH
-    )
     c = here.core
-    waited = False
-
-    def make_pair(u, block):
+
+    def make_pair(u, block, before):
         for one in (u, u + 1):
             if one >= 4:
                 units.core_copy(one - 4).wait_send()
         for shard in range(2):
             value = block(shard, 1 - c)
             for k in range(2):
-                rows = rows_at((u + k) % 4 * 2 * n + shard * n, n)
-                down[rows, pl.ds(0, n)] = value[:, k * n : (k + 1) * n].astype(bf16)
-        for one in (u - 2, u - 1):
-            if one >= 0:
-                units.first_sum(one)
-        if u == 0:
+                units.lay(u + k, shard, value[:, k * n : (k + 1) * n])
+        for one in before:
+            units.first_sum(one)
+        if u == 4:
             pl.semaphore_wait(free, 1)
         units.core_copy(u).start()
         units.core_copy(u + 1).start()
         for shard in range(2):
             value = block(shard, c)
             for k in range(2):
-                own[u + k, shard] = value[:, k * n : (k + 1) * n].astype(bf16)
+                units.keep(u + k, shard, value[:, k * n : (k + 1) * n])
 
     def make_one(u, left_side, right_side, before):
         units.core_copy(u - 4).wait_send()
         for shard in range(2):
             value = mm_tn(left_side[:, shard * n : (shard + 1) * n], right_side)
             one, two = value[:, :n], value[:, n:]
-            rows = pl.ds(u % 4 * 2 * n + shard * n, n)
-            down[rows, pl.ds(0, n)] = jnp.where(c == 0, two, one).astype(bf16)
-            own[u, shard] = jnp.where(c == 0, one, two).astype(bf16)
+            units.lay(u, shard, jnp.where(c == 0, two, one))
+            units.keep(u, shard, jnp.where(c == 0, one, two))
         for one in before:
             units.first_sum(one)
         units.core_copy(u).start()
@@ -847,15 +944,38 @@
             lambda shard, h: mm_tn(
                 active[:, cols_at(shard * 4 * n + h * 2 * n + r * n, n)], branch[...]
             ),
+            (0, 1) if r else (),
         )
+    visit(12)
+    for number in range(3):
+
+        @pl.loop(number * 4, number * 4 + 4)
+        def _(i):
+            cols = cols_at(i * tile, tile)
+            rate = bend[:, cols].astype(f32)
+            low_pre = (mm_nt(branch[...], down[rows_at(i * tile, tile), :]) * rate).astype(bf16)
+            bend[:, cols] = low_pre
+            sums_up[:, cols] = jnp.sum(low_pre.astype(f32), axis=0, keepdims=True)
+
+        if number == 0:
+            units.first_sum(2)
+            units.first_sum(3)
+        visit(32 + number)
+
+    for part in g_down:
+        part.finish()
+    pl.semaphore_signal(
+        free, inc=1, device_id=here.across(1), device_id_type=pl.DeviceIdType.MESH
+    )
     for p in range(2):
         make_pair(
             4 + 2 * p,
             lambda shard, h: mm_tn(
                 hidden[:, shard * n : (shard + 1) * n], bend[:, cols_at(h * 4 * n + p * 2 * n, 2 * n)]
             ),
+            (4, 5) if p else (),
         )
-        units.tick(p)
+        visit(13 + p)
 
     @pl.loop(0, 2 * n // ROWS)
     def _(i):
@@ -876,9 +996,10 @@
             units.first_sum(6)
             units.first_sum(7)
 
-    units.tick(2)
+        visit_one_of(i, range(15, 18))
+
     make_one(8, heads, branch[...], ())
-    units.tick(3)
+    visit(18)
     place = lax.rem(lanes, DH)
 
     @pl.loop(0, pairs)
@@ -924,26 +1045,17 @@
         def _():
             units.first_sum(8)
 
-        @pl.when(i > 0)
-        def _():
-            units.tick(3 + i)
+        visit_one_of(i, range(19, 25))
 
     for k in range(3):
         make_one(9 + k, x, active[:, k * D : (k + 1) * D], (8 + k,) if k else ())
-        if k == 1:
-            for u in range(2 * len(units.bits) + 1, 9):
-                units.put_out(u - 2 * len(units.bits) - 1)
-            units.tick(9)
+        visit(25 + k)
     units.first_sum(11)
     sums[0:1, :] = jnp.sum(active[:, 0:D].astype(f32), axis=0, keepdims=True)
     sums[1:2, :] = jnp.sum(active[:, 2 * D : 3 * D].astype(f32), axis=0, keepdims=True)
     for i in range(up.shape[1] // D):
         sums[8 + i : 9 + i, :] = sums_up[:, i * D : (i + 1) * D]
 
-    rounds = []
-    ways = [here.across(1), here.over()] + [here.across(bit) for bit in units.bits]
-    for k, way in enumerate(ways):
-        rounds.append(copies.away(sums, others.at[k], way))
     rounds[0].start()
 
     @pl.loop(0, 2 * n // ROWS)
@@ -951,26 +1063,15 @@
         rows = rows_at(i * ROWS, ROWS)
         back = second[rows, :] + mm_nt(active[rows, 0 : 3 * D], three[...])
         hidden[rows, :] = back.astype(bf16)
-
+        visit_one_of(i, range(28, 31))
+
+    layer_away.start()
+    layer_near.start()
     back_away.start()
     back_near.start()
-    units.tick(10)
-    last = UNITS + 2 * len(units.bits) + 1
-    step = 0
-    for t in range(11, last):
-        units.tick(t)
-        if step < len(rounds):
-            rounds[step].wait()
-            sums[...] += others[step]
-            step += 1
-            if step < len(rounds):
-                rounds[step].start()
-    while step < len(rounds):
-        rounds[step].wait()
-        sums[...] += others[step]
-        step += 1
-        if step < len(rounds):
-            rounds[step].start()
+    visit(31)
+    for _ in rounds:
+        next_round()
     small[0:8, :] = sums[0:8, cols_at(y * n, n)]
     for i in range(wide):
         k = i * n // D
@@ -1032,14 +1133,14 @@
         ((16, D), f32),
         ((1, wide), f32),
         ((bits + 2, 16, D), f32),
-        ((UNITS, 2, n, n), bf16),
-        ((UNITS, n, n), bf16),
+        ((UNITS, 2, 2, n // 2, n), bf16),
+        ((UNITS, 2, n // 2, n), bf16),
         *near,
-        ((UNITS, 2, n, n), bf16),
+        ((UNITS, 2, 2, n // 2, n), bf16),
         ((16, n), f32),
     ]
     anywhere = pl.BlockSpec(memory_space=pl.ANY)
-    stages = 4 + 2 * bits
+    stages = 5 + 2 * bits
     return pl.pallas_call(
         layer_kernel,
         out_shape=[jax.ShapeDtypeStruct(*kind) for kind in kinds],
@@ -1049,8 +1150,8 @@
         out_specs=[anywhere] * len(kinds),
         scratch_shapes=[pltpu.VMEM(*kind) for kind in scratch]
         + [
-            pltpu.SemaphoreType.DMA((80,)),
-            pltpu.SemaphoreType.DMA((80,)),
+            pltpu.SemaphoreType.DMA((96,)),
+            pltpu.SemaphoreType.DMA((96,)),
             pltpu.SemaphoreType.DMA((stages, UNITS)),
             pltpu.SemaphoreType.DMA((stages, UNITS)),
             pltpu.SemaphoreType.REGULAR,

time: 235 us -> 199 us (0.85)
  Pallas kernels: 220 us -> 184 us
    pallas_call x1, Pallas kernels: 218 us -> 182 us  [run_layer(): pl.pallas_call(layer_kernel, out_shape=[jax.ShapeDtypeStruct(*kind) for k...]
where the time goes in v1:
time: 199 us
  Pallas kernels  184 us (92%)
  other arithmetic  11.5 us (6%)
  local copies, waits for them, and re-layouts  3.36 us (2%)
    pallas_call x1, Pallas kernels, run_layer(): pl.pallas_call(layer_kernel, out_shape=[jax.ShapeDtypeStruct(*kind) for k...  182 us
    convert_element_type x6, other arithmetic, body(): grad.astype(f32)  11.5 us

profile of v1, /device:TPU:1, one launch (start us, length us, event | category | flops | bytes accessed | tf_op | source)
XLA Modules:
  0.0 199.1 jit_solution(278888438069525234)
XLA Ops:
  0.7 182.2 %encoder_layer.1 = (bf16[2,384,768]{2,1,0:T(8,128)(2,1)}, bf16[2,384,768]{2,1,0:T(8,128)(2,1)}, bf16[1536,768]{1,0:T(8,128)(2,1)}, bf16[384,3072]{1,0:T(8,128)(2...) custom-call(bf16[2,384,768]{2,1,0:T(8,128)(2,1)} %tokens.1, ...), custom_call_target="tpu_custom_call" | custom-call | tf_op jit(solution)/shard_map/encoder_layer/pallas_call | solution.py:1144
  182.9 1.4 split_vectors.1
  184.3 0.0 copy-start
  184.3 4.6 %convert_element_type.22 = f32[384,3072]{1,0:T(8,128)} convert(bf16[384,3072]{1,0:T(8,128)(2,1)} %get-tuple-element.47) | non-fusion elementwise | flops 1179648 | bytes 7077888 | tf_op jit(solution)/shard_map/convert_element_type | solution.py:1388
  188.9 0.0 copy-done
  188.9 0.0 copy-start.6
  188.9 2.5 %convert_element_type.23 = f32[1536,768]{1,0:T(8,128)} convert(bf16[1536,768]{1,0:T(8,128)(2,1)S(1)} %copy-done) | non-fusion elementwise | flops 1179648 | bytes 7077888 | tf_op jit(solution)/shard_map/convert_element_type | solution.py:1388
  191.4 0.0 copy-start.5
  191.4 0.0 copy-done.6
  191.4 1.1 convert_element_type.18
  192.5 0.0 copy-start.4
  192.5 0.2 copy-done.5
  192.7 1.1 convert_element_type.19
  193.8 0.0 copy-start.3
  193.8 0.0 copy-done.4
  193.8 1.1 convert_element_type.20
  194.8 0.0 copy-start.2
  194.9 0.2 copy-done.3
  195.0 1.1 convert_element_type.21
  196.1 0.3 copy-done.2
  196.4 0.0 copy-start.1
  196.4 1.0 copy.37
  197.4 0.7 copy-done.1
  198.1 1.0 copy.38
Async XLA Ops:
  184.3 4.6 %copy-start = (bf16[1536,768]{1,0:T(8,128)(2,1)S(1)}, bf16[1536,768]{1,0:T(8,128)(2,1)}, u32[]{:S(2)}) copy-start(bf16[1536,768]{1,0:T(8,128)(2,1)} %get-tuple-element.49) | copy-start | bytes 7077892
  188.9 2.6 %copy-start.6 = (bf16[384,768]{1,0:T(8,128)(2,1)S(1)}, bf16[384,768]{1,0:T(8,128)(2,1)}, u32[]{:S(2)}) copy-start(bf16[384,768]{1,0:T(8,128)(2,1)} %get-tuple-element.37) | copy-start | bytes 1769476
  191.4 1.3 copy-start.5
  192.5 1.3 copy-start.4
  193.8 1.3 copy-start.3
  194.8 1.6 copy-start.2
  196.4 1.7 copy-start.1

commit v2 on v1

--- a/solution.py
+++ b/solution.py
@@ -315,8 +315,8 @@
     def up(self, bit):
         return lax.rem(lax.div(self.rep, bit), 2)
 
-    def across(self, bit):
-        return {"rep": self.rep + bit * (1 - 2 * self.up(bit))}
+    def across(self, *bits):
+        return {"rep": self.rep + sum(bit * (1 - 2 * self.up(bit)) for bit in bits)}
 
     def over(self):
         return {"shard": 1 - self.y}
@@ -377,15 +377,15 @@
         self.hops[0].start()
         self.local.start()
 
-    def step(self):
-        if self.progress + 1 < len(self.hops):
-            self.hops[self.progress].wait_recv()
+    def step(self, k):
+        if k + 1 < len(self.hops):
+            self.hops[k].wait_recv()
+            self.hops[k + 1].start()
             self.progress += 1
-            self.hops[self.progress].start()
 
     def ready(self):
         while self.progress + 1 < len(self.hops):
-            self.step()
+            self.step(self.progress)
         self.local.wait()
         self.hops[-1].wait_recv()
 
@@ -401,44 +401,63 @@
 
 
 UNITS = 12
-WAYS = (1, 0, 1, 0, 1, 2, 1, 0, 0, 0, 0, 0)
+WAYS = (0, 1, 0, 0, 1, 0, 0, 0, 0, 0, 0, 0)
 PLAN = (
-    (3, 4),
-    (5, 3, 6, 4),
-    (7, 5, 8),
-    (9, 3, 4, 10, 6),
-    (7, 11, 9, 5),
-    (8, 6, 10),
-    (11, 7),
-    (8,),
+    (3,),
+    (),
+    (7, 5),
+    (9,),
+    (7, 11),
+    (5,),
+    (10,),
+    (11,),
+    (7, 8),
+    (),
     (9, 10),
     (11,),
     (),
     (),
-    (),
-    (),
-    (22, 23),
-    (21, 20),
-    (22, 25),
-    (21, 24, 20),
-    (22, 23),
-    (27, 21, 20, 25),
-    (22, 23, 26, 24, 21, 27),
-    (20, 25, 22, 28, 23),
-    (24, 21, 26, 27, 28),
-    (20, 25, 22, 21),
-    (21, 23, 24, 20, 26),
-    (20,),
-    (27, 22, 28),
-    (25, 23, 22),
-    (24, 25, 40, 26),
-    (29, 27),
-    (23, 28),
-    (24, 23, 29, 25, 30, 25, 26, 24, 27, 24, 28, 30, 29, 31, 26, 40, 27, 28, 27, 30, 31, 29, 26, 30, 31, 40, 26, 29, 28, 30, 28, 31, 40, 29, 30, 31, 29, 40, 29, 31, 30, 30, 31, 31),
+    (20, 22),
+    (),
+    (23, 24, 20),
+    (21, 22),
+    (),
+    (20, 23, 25, 21),
+    (20, 22),
+    (20, 23, 25, 26),
+    (21, 22, 27, 26),
+    (21, 23, 24),
+    (21, 22, 25, 28, 26),
+    (22, 27),
+    (24,),
+    (23, 25),
+    (23, 26, 28, 40, 25, 29),
+    (25, 27),
+    (),
+    (26, 24, 26, 30, 29, 28, 24, 27, 24, 31, 30, 29, 27, 28, 27, 31, 30, 28, 29, 28, 31, 40, 29, 40, 30, 29, 40, 31, 30, 30, 40, 31, 31),
     (),
     (),
     (20, 21),
+    (),
+    (),
+    (),
+    (),
+    (),
+    (4,),
+    (5,),
+    (3, 6),
+    (4,),
+    (8,),
+    (),
+    (3,),
+    (4, 10, 6),
+    (),
+    (9,),
+    (8,),
+    (6,),
 )
+ORDER = [0] + [place for i in range(6) for place in (40 + 2 * i, 41 + 2 * i, 1 + i)]
+ORDER += [*range(7, 13), 32, 33, 34, *range(13, 32)]
 
 
 class Units:
@@ -453,13 +472,17 @@
             self.all_bits.append(bit)
             bit *= 2
         self.progress = [0] * UNITS
-        self.stages = 3 + 2 * len(self.all_bits)
-
-    def bits(self, u):
-        bits = list(self.all_bits)
-        if WAYS[u] == 2 and len(bits) > 1:
-            bits[0], bits[1] = bits[1], bits[0]
-        return bits
+        depth = self.all_bits[1:]
+        self.parts = 1 << len(depth)
+        self.others = {}
+        self.place = sum((here.up(bit) << k for k, bit in enumerate(depth)), 0)
+        for j in range(1, self.parts):
+            flips = [bit for k, bit in enumerate(depth) if j >> k & 1]
+            place = 0
+            for k, bit in enumerate(depth):
+                up = here.up(bit)
+                place = place + (1 - up if j >> k & 1 else up) * (1 << k)
+            self.others[j] = (here.across(*flips), place)
 
     def copy(self, stage, u, source, target, peer):
         return pltpu.make_async_remote_copy(
@@ -499,40 +522,34 @@
 
     def away_copy(self, k, u):
         y, own, here = self.here.y, self.own, self.here
-        bits = self.bits(u)
-        up = here.up(bits[0])
-        first_y = WAYS[u] == 0
-        if k == 0 and first_y:
+        up = here.up(2)
+        if k == 0 and WAYS[u] == 0:
             return self.copy(1, u, own.at[u, 1 - y], self.far.at[u], here.over())
         if k == 0:
-            return self.copy(1, u, own.at[u, :, 1 - up], self.far.at[u], here.across(bits[0]))
-        if k == 1 and first_y:
-            return self.copy(2, u, own.at[u, y, 1 - up], self.near[0].at[u], here.across(bits[0]))
-        if k == 1:
-            return self.copy(2, u, own.at[u, 1 - y, up], self.near[0].at[u], here.over())
-        start, size = self.inner(u, k - 2)
-        half = size // 2
-        rows = rows_at(start + (1 - here.up(bits[k - 1])) * half, half)
-        return self.copy(
-            1 + k, u, own.at[u, y, up, rows, :], self.near[k - 1].at[u], here.across(bits[k - 1])
-        )
-
-    def inner(self, u, level):
-        size, start = self.n // 2, 0
-        for bit in self.bits(u)[1 : 1 + level]:
-            size //= 2
-            start = start + self.here.up(bit) * size
-        return start, size
+            return self.copy(1, u, own.at[u, :, 1 - up], self.far.at[u], here.across(2))
+        if WAYS[u] == 0:
+            return self.copy(2, u, own.at[u, y, 1 - up], self.near[0].at[u], here.across(2))
+        return self.copy(2, u, own.at[u, 1 - y, up], self.near[0].at[u], here.over())
+
+    def rows(self, place):
+        size = self.n // 2 // self.parts
+        return rows_at(place * size, size)
+
+    def out_copy(self, j, u):
+        peer, place = self.others[j]
+        source = self.own.at[u, self.here.y, self.here.up(2), self.rows(place), :]
+        return self.copy(2 + j, u, source, self.near[1].at[u, j - 1], peer)
+
+    def in_copy(self, j, u):
+        peer, _ = self.others[j]
+        piece = self.done.at[u, self.here.core, self.here.up(2), self.rows(self.place), :]
+        return self.copy(1 + self.parts + j, u, piece, piece, peer)
 
     def back_copy(self, k, u):
-        bits = self.bits(u)
-        level = len(bits) - k
         piece = self.done.at[u, self.here.core]
-        bit = bits[level - 1] if level else 1
-        if level:
-            start, size = self.inner(u, level - 1)
-            piece = self.done.at[u, self.here.core, self.here.up(bits[0]), rows_at(start, size), :]
-        return self.copy(2 + len(bits) + k, u, piece, piece, self.here.across(bit))
+        if k == 0:
+            piece = piece.at[self.here.up(2)]
+        return self.copy(1 + 2 * self.parts + k, u, piece, piece, self.here.across(1 if k else 2))
 
     def out_copies(self, u):
         n = self.n
@@ -547,7 +564,7 @@
                 else:
                     place = square[u - 8].at[pl.ds(rows, n // 2), pl.ds(h * n, n)]
                 yield pltpu.make_async_copy(
-                    self.done.at[u, h, part], place, (self.send, self.recv)[h].at[self.stages + part, u]
+                    self.done.at[u, h, part], place, (self.send, self.recv)[h].at[3 + 2 * self.parts + part, u]
                 )
 
     def keep(self, u, shard, value):
@@ -557,7 +574,7 @@
 
     def first_sum(self, u):
         y = self.here.y
-        up = self.here.up(self.bits(u)[0])
+        up = self.here.up(2)
         self.core_copy(u).wait_recv()
         if WAYS[u] == 0:
             order = [(1 - y, 0), (1 - y, 1), (y, 0), (y, 1)]
@@ -569,17 +586,13 @@
             if number == 1:
                 self.away_copy(0, u).start()
 
-    def step(self, u):
-        bits = len(self.all_bits)
-        k = self.progress[u]
-        if k > 2 * bits + 1:
+    def step(self, u, k):
+        if k == 6:
             return
-        self.progress[u] = k + 1
-        y, own = self.here.y, self.own
-        up = self.here.up(self.bits(u)[0])
-        if k <= bits:
-            self.away_copy(k, u).wait_recv()
+        self.progress[u] += 1
+        y, own, up = self.here.y, self.own, self.here.up(2)
         if k == 0:
+            self.away_copy(0, u).wait_recv()
             if WAYS[u] == 0:
                 order = [((y, 1 - up), 1 - up), ((y, up), up)]
             else:
@@ -589,40 +602,48 @@
                 own[u, shard, part] = (own[u, shard, part].astype(f32) + theirs).astype(bf16)
                 if number == 0:
                     self.away_copy(1, u).start()
-        elif k < bits:
-            start, size = self.inner(u, k - 1)
-            half = size // 2
-            side = self.here.up(self.bits(u)[k])
-            for number, part in enumerate((1 - side, side)):
-                rows = rows_at(start + part * half, half)
-                theirs = self.near[k - 1][u, rows_at(part * half, half), :].astype(f32)
+        elif k == 1:
+            self.away_copy(1, u).wait_recv()
+            for j in list(self.others) + [0]:
+                rows = self.rows(self.others[j][1] if j else self.place)
+                theirs = self.near[0][u, rows, :].astype(f32)
                 own[u, y, up, rows, :] = (own[u, y, up, rows, :].astype(f32) + theirs).astype(bf16)
-                if number == 0:
-                    self.away_copy(k + 1, u).start()
-        elif k == bits:
-            start, size = self.inner(u, k - 1)
-            total = own[u, y, up, rows_at(start, size), :].astype(f32)
-            total = total + self.near[k - 1][u].astype(f32)
-            self.done[u, self.here.core, up, rows_at(start, size), :] = total.astype(bf16)
+                if j:
+                    self.out_copy(j, u).start()
+        elif k == 2:
+            rows = self.rows(self.place)
+            total = own[u, y, up, rows, :].astype(f32)
+            for j in self.others:
+                self.out_copy(j, u).wait_recv()
+                total = total + self.near[1][u, j - 1].astype(f32)
+            self.done[u, self.here.core, up, rows, :] = total.astype(bf16)
+            for j in self.others:
+                self.in_copy(j, u).start()
+        elif k == 3:
+            for j in self.others:
+                self.in_copy(j, u).wait_recv()
             self.back_copy(0, u).start()
+        elif k == 4:
+            self.back_copy(0, u).wait_recv()
+            self.back_copy(1, u).start()
         else:
-            self.back_copy(k - bits - 1, u).wait_recv()
-            if k <= 2 * bits:
-                self.back_copy(k - bits, u).start()
-            else:
-                for copy in self.out_copies(u):
-                    copy.start()
+            self.back_copy(1, u).wait_recv()
+            for copy in self.out_copies(u):
+                copy.start()
 
     def finish(self):
         for u in range(UNITS):
-            while self.progress[u] <= 2 * len(self.all_bits) + 1:
-                self.step(u)
+            while self.progress[u] < 6:
+                self.step(u, self.progress[u])
         for u in range(UNITS):
             if u >= UNITS - 4:
                 self.core_copy(u).wait_send()
-            for k in range(len(self.all_bits) + 1):
+            for k in range(2):
                 self.away_copy(k, u).wait_send()
                 self.back_copy(k, u).wait_send()
+            for j in self.others:
+                self.out_copy(j, u).wait_send()
+                self.in_copy(j, u).wait_send()
             for copy in self.out_copies(u):
                 copy.wait()
 
@@ -677,9 +698,8 @@
     others,
     own,
     far,
-    near_x,
-    near_z,
-    near_w,
+    near_one,
+    near_two,
     done,
     small,
     send,
@@ -693,7 +713,7 @@
     copies = Copies(send, recv)
     n = w_query.shape[0]
     y = here.y
-    near = (near_x, near_z, near_w)
+    near = (near_one, near_two)
     o_layer, o_back, *o_grads, o_small = outs
     units = Units(here, reps, unit_send, unit_recv, down, own, far, near, done, o_grads)
     peers = [here.over(), here.across(1)] + [here.across(bit) for bit in units.all_bits]
@@ -768,9 +788,9 @@
     sums[...] = jnp.zeros_like(sums)
     lse[...] = jnp.zeros_like(lse)
 
-    for _ in range(3):
+    for k in range(3):
         for part in g_three:
-            part.step()
+            part.step(k)
     vec_away.wait_recv()
     for half in range(2):
         table = raw_vectors[half]
@@ -813,17 +833,26 @@
             if k + 1 < len(rounds):
                 rounds[k + 1].start()
 
+    numbered, count = {}, {}
+    for place in ORDER:
+        numbered[place] = []
+        for one in PLAN[place]:
+            numbered[place].append((one, count.get(one, 0)))
+            count[one] = count.get(one, 0) + 1
+
     def visit(place):
-        for one in PLAN[place]:
+        for one, k in numbered[place]:
             if one == 40:
                 next_round()
             elif one >= 20:
-                units.step(one - 20)
+                units.step(one - 20, k)
             else:
-                pieces[one].step()
+                pieces[one].step(k)
 
     def visit_one_of(i, places):
         for number, place in enumerate(places):
+            if not PLAN[place]:
+                continue
 
             @pl.when(i == number)
             def _():
@@ -857,8 +886,8 @@
                 total_lse = jnp.where(lanes == 2 * i + number, top + jnp.log(sum_all), total_lse)
             lse[rows, :] = total_lse
             heads[rows, cols_at(i * PAIR, PAIR)] = jnp.where(left, outs[0], outs[1]).astype(bf16)
-
-        visit_one_of(i, range(1, 7))
+            turn = start // ROWS
+            visit_one_of(i, range(40 + turn, 52, 2) if turn < 2 else range(1, 7))
 
     g_attn.ready()
 
@@ -1058,17 +1087,18 @@
 
     rounds[0].start()
 
-    @pl.loop(0, 2 * n // ROWS)
-    def _(i):
-        rows = rows_at(i * ROWS, ROWS)
+    for number in range(2):
+        rows = pl.ds((1 - number) * n, n)
         back = second[rows, :] + mm_nt(active[rows, 0 : 3 * D], three[...])
         hidden[rows, :] = back.astype(bf16)
-        visit_one_of(i, range(28, 31))
-
+        if number == 0:
+            back_away.start()
+        visit(28 + number)
+
+    back_near.start()
+    visit(30)
     layer_away.start()
     layer_near.start()
-    back_away.start()
-    back_near.start()
     visit(31)
     for _ in rounds:
         next_round()
@@ -1106,7 +1136,8 @@
         ((n, D), bf16),
         ((16, n), f32),
     ]
-    near = [((UNITS, max(16, n >> (k + 1)), n), bf16) for k in range(3)]
+    parts = reps // 4
+    near = [((UNITS, n // 2, n), bf16), ((UNITS, max(1, parts - 1), n // 2 // parts, n), bf16)]
     scratch = [
         ((count, D), bf16),
         ((count, D), bf16),
@@ -1140,7 +1171,7 @@
         ((16, n), f32),
     ]
     anywhere = pl.BlockSpec(memory_space=pl.ANY)
-    stages = 5 + 2 * bits
+    stages = 5 + 2 * parts
     return pl.pallas_call(
         layer_kernel,
         out_shape=[jax.ShapeDtypeStruct(*kind) for kind in kinds],
@@ -1163,25 +1194,45 @@
     )(tokens, cotangent, seq, *lines, b_up, *weights)
 
 
-def split_vectors(table, *outs):
-    *lines, b_up = outs
+STEPS = 2
+
+
+def finish_kernel(*refs):
+    table = refs[8]
+    for source, target in zip(refs[:8], refs[9:17]):
+        target[...] = source[...].astype(target.dtype)
+    *lines, b_up = refs[17:]
     n = table.shape[1]
-    for i, line in enumerate(lines):
-        line[...] = table[i : i + 1, :].reshape(n)
-    for i in range(b_up.shape[0] // n):
-        b_up[pl.ds(i * n, n)] = table[8 + i : 9 + i, :].reshape(n)
-
-
-def run_split(table, wide):
+
+    @pl.when(pl.program_id(0) == 0)
+    def _():
+        for i, line in enumerate(lines):
+            line[...] = table[i : i + 1, :].reshape(n)
+        for i in range(b_up.shape[0] // n):
+            b_up[pl.ds(i * n, n)] = table[8 + i : 9 + i, :].reshape(n)
+
+
+def run_finish(arrays, table, wide):
     n = table.shape[1]
-    inside = pl.BlockSpec(memory_space=pltpu.VMEM)
+    inside = pl.BlockSpec(table.shape, lambda i: (0, 0))
+
+    def blocks(array):
+        if array.ndim == 3:
+            return pl.BlockSpec((2, array.shape[1] // STEPS, array.shape[2]), lambda i: (0, i, 0))
+        return pl.BlockSpec((array.shape[0] // STEPS, array.shape[1]), lambda i: (i, 0))
+
+    kinds = [bf16] * 2 + [f32] * 6
+    lines = [n] * 8 + [wide * n]
+    specs = [blocks(array) for array in arrays]
     return pl.pallas_call(
-        split_vectors,
-        out_shape=[jax.ShapeDtypeStruct((n,), f32)] * 8 + [jax.ShapeDtypeStruct((wide * n,), f32)],
-        in_specs=[inside],
-        out_specs=[inside] * 9,
-        name="split_vectors",
-    )(table)
+        finish_kernel,
+        grid=(STEPS,),
+        out_shape=[jax.ShapeDtypeStruct(a.shape, kind) for a, kind in zip(arrays, kinds)]
+        + [jax.ShapeDtypeStruct((size,), f32) for size in lines],
+        in_specs=specs + [inside],
+        out_specs=specs + [pl.BlockSpec((size,), lambda i: (0,)) for size in lines],
+        name="finish",
+    )(*arrays, table)
 
 
 def general_body(
@@ -1376,7 +1427,7 @@
     part = w_query.shape[0]
     wide = b_up.shape[0] // part
     lines = [b_query, b_value, b_attn, norm_gain, norm_bias, b_down, out_gain, out_bias]
-    layer, back, *grads, small = run_layer(
+    *arrays, small = run_layer(
         tokens,
         cotangent,
         seq_lengths,
@@ -1385,8 +1436,8 @@
         (w_query, w_key, w_value, w_attn, w_up, w_down),
         reps,
     )
-    g_down, g_up, g_attn, g_query, g_key, g_value = [grad.astype(f32) for grad in grads]
-    d_query, d_value, d_attn, d_gain, d_bias, d_down, d_out_gain, d_out_bias, d_up = run_split(small, wide)
+    layer, back, g_down, g_up, g_attn, g_query, g_key, g_value, *lines = run_finish(arrays, small, wide)
+    d_query, d_value, d_attn, d_gain, d_bias, d_down, d_out_gain, d_out_bias, d_up = lines
     return (
         layer,
         back,

time: 199 us -> 190 us (0.955)
  other arithmetic: 11.5 us -> 0 us
  Pallas kernels: 184 us -> 189 us
  local copies, waits for them, and re-layouts: 3.36 us -> 0 us
    convert_element_type x6 -> x0, other arithmetic: 11.5 us -> none  [body(): grad.astype(f32)]
    pallas_call x1, Pallas kernels: 1.37 us -> 8.7 us  [run_finish(): pl.pallas_call(finish_kernel, grid=(STEPS,), out_shape=[jax.ShapeDtypeStr...]
    unnamed x16 -> x0, local copies, waits for them, and re-layouts: 3.36 us -> none
    pallas_call x1, Pallas kernels: 182 us -> 180 us  [run_layer(): pl.pallas_call(layer_kernel, out_shape=[jax.ShapeDtypeStruct(*kind) for k...]
where the time goes in v2:
time: 190 us
  Pallas kernels  189 us (99%)
    pallas_call x1, Pallas kernels, run_layer(): pl.pallas_call(layer_kernel, out_shape=[jax.ShapeDtypeStruct(*kind) for k...  180 us
    pallas_call x1, Pallas kernels, run_finish(): pl.pallas_call(finish_kernel, grid=(STEPS,), out_shape=[jax.ShapeDtypeStr...  8.7 us

profile of v2, /device:TPU:1, one launch (start us, length us, event | category | flops | bytes accessed | tf_op | source)
XLA Modules:
  0.0 189.8 jit_solution(2383280132319601404)
XLA Ops:
  0.7 180.3 %encoder_layer.1 = (bf16[2,384,768]{2,1,0:T(8,128)(2,1)}, bf16[2,384,768]{2,1,0:T(8,128)(2,1)}, bf16[1536,768]{1,0:T(8,128)(2,1)}, bf16[384,3072]{1,0:T(8,128)(2...) custom-call(bf16[2,384,768]{2,1,0:T(8,128)(2,1)} %tokens.1, ...), custom_call_target="tpu_custom_call" | custom-call | tf_op jit(solution)/shard_map/encoder_layer/pallas_call | solution.py:1175
  180.9 8.7 %finish.1 = (bf16[2,384,768]{2,1,0:T(8,128)(2,1)}, bf16[2,384,768]{2,1,0:T(8,128)(2,1)}, f32[1536,768]{1,0:T(8,128)}, f32[384,3072]{1,0:T(8,128)}, f32[384,768]{...) custom-call(bf16[2,384,768]{2,1,0:T(8,128)(2,1)} %get-tuple-element., ...), custom_call_target="tpu_custom_call" | custom-call | tf_op jit(solution)/shard_map/finish/pallas_call | solution.py:1227
